TPU v7x, 256 devices: a whole 4x4x8 slice. The times are simulated.
256 devices in a mesh: section: 16 (over y_hi, z), fsdp: 16 (over x, y_lo, core).
Axes of the slice: x: 4, y: 4 (y_hi: 2, y_lo: 2; y = y_hi * 2 + y_lo), z: 8, core: 2. Of those that a mesh axis runs over, the one named last changes fastest.
Arguments:
- branch_in: bfloat16 [16, 8192, 128], P('section', 'fsdp'), may hold values from -0.0625 to 0.0625
- branch_out: bfloat16 [16, 128, 8192], P('section', None, 'fsdp'), may hold values from -0.5 to 0.5
- down_inputs: bfloat16 [16, 12, 128, 8192], P('section', None, 'fsdp'), may hold values from -6 to 6
- up_inputs: bfloat16 [16, 12, 128, 8192], P('section', None, 'fsdp'), may hold values from -6 to 6
- top_grads: bfloat16 [2, 12, 128, 8192], P(None, None, 'fsdp'), may hold values from -6 to 6
- plan: int32 [2, 12], replicated, may hold values from 0 to 11, each once within a row
- reward_pos: int32 [2, 12, 16], replicated, may hold values from 0 to 7
- reward_cot: float32 [2, 12, 16], replicated, may hold values from -4 to 4
- reward_head: float32 [8192], replicated, may hold values from -5 to 5
Outputs:
- grad_in: float32 [16, 8192, 128], P('section', 'fsdp')
- grad_out: float32 [16, 128, 8192], P('section', None, 'fsdp')
Inputs may be any that keep to these rules, and one draw needn't show every extreme that they name: Each row of plan names every microbatch once.
All inputs are finite; a program needn't handle non-finite values.
Results may differ from a plain program's by a relative error of at most 0.03.
Values may be sent and summed in bfloat16 or wider, within the bound.
No kernel may reach another device: no remote copies, remote signals or barrier semaphores. Data moves between devices by JAX's collectives and lax.ppermute only.
A program may use at most 128 MiB of HBM per device.

v0:
```python
import jax
import jax.numpy as jnp
from jax import lax
from jax.sharding import PartitionSpec as P


def from_partner(value, axis, apart):
    mask = 2**apart
    pairs = [(source, source ^ mask) for source in range(lax.axis_size(axis))]
    return lax.ppermute(value, axis, pairs)


def passed_along(value, axis, steps):
    count = lax.axis_size(axis)
    initial, last = (max(0, -steps), min(count, count - steps))
    return lax.ppermute(value, axis, [(source, source + steps) for source in range(initial, last)])


def branch_grads(inputs, grad, w_in, w_out):
    pre_act = jnp.dot(inputs, w_in, preferred_element_type=jnp.float32)
    sig_val = jax.nn.sigmoid(pre_act)
    hidden = (pre_act * sig_val).astype(jnp.bfloat16)
    grad_hidden = lax.dot_general(
        grad, w_out, (((1,), (1,)), ((), ())), preferred_element_type=jnp.float32
    )
    grad_pre = (grad_hidden * sig_val * (1.0 + pre_act * (1.0 - sig_val))).astype(jnp.bfloat16)
    back_term = lax.dot_general(
        grad_pre, w_in, (((1,), (1,)), ((), ())), preferred_element_type=jnp.float32
    )
    back = (grad.astype(jnp.float32) + back_term).astype(jnp.bfloat16)
    return (hidden, grad_pre, back)


def bit_order(count):
    return list(range(count))


def fetch_mirror(packed):
    hops = lax.axis_size("section").bit_length() - 1
    for bit_index in bit_order(hops):
        packed = from_partner(packed, "section", bit_index)
    return packed


def send_mirror(packed):
    hops = lax.axis_size("section").bit_length() - 1
    for bit_index in bit_order(hops):
        packed = from_partner(packed.astype(jnp.bfloat16), "section", bit_index).astype(
            packed.dtype
        )
    return packed


def slot_pass(
    slot,
    starting,
    received,
    inputs,
    top,
    order,
    positions,
    rewards,
    head,
    row_global,
    seq_len,
    w_in,
    w_out,
    state,
):
    micro_count = inputs.shape[0]
    valid = jnp.logical_and(slot >= 0, slot < micro_count)
    clipped = jnp.clip(slot, 0, micro_count - 1)

    def active(operands):
        acc_in, acc_out = operands
        ident = lax.dynamic_index_in_dim(order, clipped, 0, keepdims=False)
        picked = jnp.arange(micro_count, dtype=jnp.int32) == ident
        pos_now = jnp.sum(jnp.where(picked[:, None], positions, 0), axis=0)
        cot_now = jnp.sum(jnp.where(picked[:, None], rewards, 0.0), axis=0)
        target = jnp.arange(positions.shape[1], dtype=jnp.int32) * seq_len + pos_now
        row_weight = jnp.sum(
            jnp.where(target[:, None] == row_global[None, :], cot_now[:, None], 0.0), axis=0
        )
        top_now = lax.dynamic_index_in_dim(top, clipped, 0, keepdims=False)
        first_grad = (top_now.astype(jnp.float32) + row_weight[:, None] * head[None, :]).astype(
            jnp.bfloat16
        )
        grad = jnp.where(starting, first_grad, received)
        rows_in = lax.dynamic_index_in_dim(inputs, ident, 0, keepdims=False)
        hidden, grad_pre, back = branch_grads(rows_in, grad, w_in, w_out)
        acc_in = acc_in + lax.dot_general(
            rows_in, grad_pre, (((0,), (0,)), ((), ())), preferred_element_type=jnp.float32
        )
        acc_out = acc_out + lax.dot_general(
            hidden, grad, (((0,), (0,)), ((), ())), preferred_element_type=jnp.float32
        )
        return ((acc_in, acc_out), back)

    def resting(operands):
        return (operands, jnp.zeros_like(received))

    return lax.cond(valid, active, resting, state)


def on_device(
    branch_in,
    branch_out,
    down_inputs,
    up_inputs,
    top_grads,
    plan,
    reward_pos,
    reward_cot,
    reward_head,
):
    section_count = lax.axis_size("section")
    section_idx = lax.axis_index("section")
    fsdp_count = lax.axis_size("fsdp")
    micro_count = down_inputs.shape[1]
    local_rows = down_inputs.shape[2]
    width = down_inputs.shape[3]
    seq_count = reward_pos.shape[2]
    seq_len = local_rows * fsdp_count // seq_count
    row_global = lax.axis_index("fsdp") * local_rows + jnp.arange(local_rows, dtype=jnp.int32)
    own_in_shard = branch_in[0]
    own_out_shard = branch_out[0]
    packed_own = jnp.stack([own_in_shard.reshape(own_out_shard.shape), own_out_shard])
    packed_far = fetch_mirror(packed_own)
    far_in_shard = packed_far[0].reshape(own_in_shard.shape)
    far_out_shard = packed_far[1]
    own_in, own_out = (
        lax.all_gather(own_in_shard, "fsdp", axis=0, tiled=True),
        lax.all_gather(own_out_shard, "fsdp", axis=1, tiled=True),
    )
    far_in, far_out = (
        lax.all_gather(far_in_shard, "fsdp", axis=0, tiled=True),
        lax.all_gather(far_out_shard, "fsdp", axis=1, tiled=True),
    )
    zero_in = jnp.zeros(own_in.shape, jnp.float32)
    zero_out = jnp.zeros(own_out.shape, jnp.float32)
    zero_rows = jnp.zeros((local_rows, width), jnp.bfloat16)
    down_state = (zero_in, zero_out)
    up_state = (zero_in, zero_out)

    def advance(step_idx, carry):
        recv_down, recv_up, state_down, state_up = carry
        slot_down = step_idx - (section_count - 1 - section_idx)
        slot_up = step_idx - section_idx
        state_down, back_down = slot_pass(
            slot_down,
            section_idx == section_count - 1,
            recv_down,
            down_inputs[0],
            top_grads[0],
            plan[0],
            reward_pos[0],
            reward_cot[0],
            reward_head,
            row_global,
            seq_len,
            own_in,
            own_out,
            state_down,
        )
        state_up, back_up = slot_pass(
            slot_up,
            section_idx == 0,
            recv_up,
            up_inputs[0],
            top_grads[1],
            plan[1],
            reward_pos[1],
            reward_cot[1],
            reward_head,
            row_global,
            seq_len,
            far_in,
            far_out,
            state_up,
        )
        recv_down = passed_along(back_down, "section", -1)
        recv_up = passed_along(back_up, "section", 1)
        return (recv_down, recv_up, state_down, state_up)

    carry = lax.fori_loop(
        0, section_count + micro_count - 1, advance, (zero_rows, zero_rows, down_state, up_state)
    )
    state_down = carry[2]
    state_up = carry[3]
    shares = (
        lax.psum_scatter(
            state_down[0].astype(jnp.bfloat16), "fsdp", scatter_dimension=0, tiled=True
        ).astype(jnp.float32),
        lax.psum_scatter(
            state_down[1].astype(jnp.bfloat16), "fsdp", scatter_dimension=1, tiled=True
        ).astype(jnp.float32),
        lax.psum_scatter(
            state_up[0].astype(jnp.bfloat16), "fsdp", scatter_dimension=0, tiled=True
        ).astype(jnp.float32),
        lax.psum_scatter(
            state_up[1].astype(jnp.bfloat16), "fsdp", scatter_dimension=1, tiled=True
        ).astype(jnp.float32),
    )
    packed_up = jnp.stack([shares[2].reshape(shares[3].shape), shares[3]])
    packed_back = send_mirror(packed_up)
    grad_in = shares[0] + packed_back[0].reshape(shares[0].shape)
    grad_out = shares[1] + packed_back[1]
    return (grad_in[None], grad_out[None])


def solution(mesh):
    in_specs = (
        P("section", "fsdp", None),
        P("section", None, "fsdp"),
        P("section", None, "fsdp", None),
        P("section", None, "fsdp", None),
        P(None, None, "fsdp", None),
        P(),
        P(),
        P(),
        P(),
    )
    out_specs = (P("section", "fsdp", None), P("section", None, "fsdp"))
    return jax.shard_map(
        on_device, mesh=mesh, in_specs=in_specs, out_specs=out_specs, check_vma=False
    )
```

profile of v0, /device:TPU:16, one launch (start us, length us, event | category | flops | bytes accessed | tf_op | source)
XLA Modules:
  0.0 1438.2 jit_solution(11273259088735241867)
XLA Ops:
  12.6 6.3 collective-permute-done.2
  22.2 11.2 collective-permute-done.3
  39.7 11.7 collective-permute-done.4
  51.7 7.5 collective-permute-done.5
  61.6 25.2 %all-gather.10.cloned.1.call-done = bf16[1,128,8192]{2,1,0:T(8,128)(2,1)} async-done(((bf16[1,128,512]{2,1,0:T(8,128)(2,1)}), bf16[1,128,8192]{2,1,0:T(8,128)(2,1)}) %all-gather.10.cloned.1.call-update) | async-done | bytes 2097168 | tf_op jit(solution)/shard_map/all_gather | solution.py:133
  86.9 38.9 %all-gather.8.cloned.1.call-done = bf16[8192,128]{1,0:T(8,128)(2,1)} async-done(((bf16[512,128]{1,0:T(8,128)(2,1)}), bf16[8192,128]{1,0:T(8,128)(2,1)}) %all-gather.8.cloned.1.call-update) | async-done | bytes 2097168 | tf_op jit(solution)/shard_map/all_gather | solution.py:136
  125.7 38.6 %all-gather.14.cloned.1.call-done = bf16[1,128,8192]{2,1,0:T(8,128)(2,1)} async-done(((bf16[1,128,512]{2,1,0:T(8,128)(2,1)}), bf16[1,128,8192]{2,1,0:T(8,128)(2,1)}) %all-gather.14.cloned.1.call-update) | async-done | bytes 2097168 | tf_op jit(solution)/shard_map/all_gather | solution.py:137
  173.9 920.0 %while.25 = (s32[]{:T(128)}, bf16[8,8192]{1,0:T(8,128)(2,1)S(1)}, bf16[8,8192]{1,0:T(8,128)(2,1)S(1)}, f32[8192,128]{1,0:T(8,128)}, f32[128,8192]{1,0:T(8,128)},...) while((s32[]{:T(128)}, bf16[8,8192]{1,0:T(8,128)(2,1)S(1)}, ...), condition=%wide.region_11.12_spmd.clone, body=%wide.region_0.11_spmd.clone.sunk | while | flops 173046048 | bytes 206939488 | solution.py:185
  182.5 7.8 collective-permute-done.1
  234.7 19.0 %collective-permute-done.1 = bf16[8,8192]{1,0:T(8,128)(2,1)S(1)} collective-permute-done((bf16[8,8192]{1,0:T(8,128)(2,1)S(1)}, bf16[8,8192]{1,0:T(8,128)(2,1)S(1)}, u32[]{:S(2)}, u32[]{:S(2)}) %collective-permute-start.1) | collective-permute-done | bytes 131104 | tf_op jit(solution)/shard_map/while/body/eval_jaxpr/ppermute | solution.py:16
  253.7 21.6 %collective-permute-start = (bf16[8,8192]{1,0:T(8,128)(2,1)S(1)}, bf16[8,8192]{1,0:T(8,128)(2,1)S(1)}, u32[]{:S(2)}, u32[]{:S(2)}) collective-permute-start(bf16[8,8192]{1,0:T(8,128)(2,1)S(1)} %get-tuple-element.853), channel_id=1, source_target_pairs={{16,0},{32,16},{48,32},{64,48},{80,64},{96,80},{112,96},{128,112},... | collective-permute-start | bytes 393224 | tf_op jit(solution)/shard_map/while/body/eval_jaxpr/ppermute | solution.py:16
  277.7 22.3 %collective-permute-done.1 = bf16[8,8192]{1,0:T(8,128)(2,1)S(1)} collective-permute-done((bf16[8,8192]{1,0:T(8,128)(2,1)S(1)}, bf16[8,8192]{1,0:T(8,128)(2,1)S(1)}, u32[]{:S(2)}, u32[]{:S(2)}) %collective-permute-start.1) | collective-permute-done | bytes 131104 | tf_op jit(solution)/shard_map/while/body/eval_jaxpr/ppermute | solution.py:16
  300.1 21.9 %collective-permute-start = (bf16[8,8192]{1,0:T(8,128)(2,1)S(1)}, bf16[8,8192]{1,0:T(8,128)(2,1)S(1)}, u32[]{:S(2)}, u32[]{:S(2)}) collective-permute-start(bf16[8,8192]{1,0:T(8,128)(2,1)S(1)} %get-tuple-element.853), channel_id=1, source_target_pairs={{16,0},{32,16},{48,32},{64,48},{80,64},{96,80},{112,96},{128,112},... | collective-permute-start | bytes 393224 | tf_op jit(solution)/shard_map/while/body/eval_jaxpr/ppermute | solution.py:16
  322.0 19.6 %collective-permute-start.1 = (bf16[8,8192]{1,0:T(8,128)(2,1)S(1)}, bf16[8,8192]{1,0:T(8,128)(2,1)S(1)}, u32[]{:S(2)}, u32[]{:S(2)}) collective-permute-start(bf16[8,8192]{1,0:T(8,128)(2,1)S(1)} %get-tuple-element.854), channel_id=1, source_target_pairs={{0,16},{16,32},{32,48},{48,64},{64,80},{80,96},{96,112},{112,128},... | collective-permute-start | bytes 393224 | tf_op jit(solution)/shard_map/while/body/eval_jaxpr/ppermute | solution.py:16
  348.0 16.6 %conditional.6 = (f32[8192,128]{1,0:T(8,128)}, f32[128,8192]{1,0:T(8,128)}, bf16[8,8192]{1,0:T(8,128)(2,1)S(1)}) conditional(s32[]{:T(128)} %convert_element_type.119, (f32[8192,128]{1,0:T(8,128)}, f32[128,8192]{1,0:T(8,128)}) %tuple.66, (s32[2,12]{1,0:T(2,128)S(1)}, s32[]{:T(128)}, bf16[1,12,8,8192]{3,2,1,0:T(8,128)(2,1)}, pred[]{:T(512)}, ...), branch_computations={%region_1.1_spmd, %region_2.5_spmd} | conditional | flops 86523016 | bytes 102945120 | solution.py:102
  372.4 22.3 %collective-permute-done.1 = bf16[8,8192]{1,0:T(8,128)(2,1)S(1)} collective-permute-done((bf16[8,8192]{1,0:T(8,128)(2,1)S(1)}, bf16[8,8192]{1,0:T(8,128)(2,1)S(1)}, u32[]{:S(2)}, u32[]{:S(2)}) %collective-permute-start.1) | collective-permute-done | bytes 131104 | tf_op jit(solution)/shard_map/while/body/eval_jaxpr/ppermute | solution.py:16
  394.8 16.6 %conditional.6 = (f32[8192,128]{1,0:T(8,128)}, f32[128,8192]{1,0:T(8,128)}, bf16[8,8192]{1,0:T(8,128)(2,1)S(1)}) conditional(s32[]{:T(128)} %convert_element_type.119, (f32[8192,128]{1,0:T(8,128)}, f32[128,8192]{1,0:T(8,128)}) %tuple.66, (s32[2,12]{1,0:T(2,128)S(1)}, s32[]{:T(128)}, bf16[1,12,8,8192]{3,2,1,0:T(8,128)(2,1)}, pred[]{:T(512)}, ...), branch_computations={%region_1.1_spmd, %region_2.5_spmd} | conditional | flops 86523016 | bytes 102945120 | solution.py:102
  415.3 18.0 %conditional.7 = (f32[8192,128]{1,0:T(8,128)}, f32[128,8192]{1,0:T(8,128)}, bf16[8,8192]{1,0:T(8,128)(2,1)S(1)}) conditional(s32[]{:T(128)} %convert_element_type.120, (f32[8192,128]{1,0:T(8,128)}, f32[128,8192]{1,0:T(8,128)}) %tuple.68, (s32[2,12]{1,0:T(2,128)S(1)}, s32[]{:T(128)}, bf16[1,12,8,8192]{3,2,1,0:T(8,128)(2,1)}, pred[]{:T(512)}, ...), branch_computations={%region_6.6_spmd, %region_7.10_spmd} | conditional | flops 86523016 | bytes 102945120 | solution.py:102
  435.2 8.5 collective-permute-done.1
  443.7 16.6 %conditional.6 = (f32[8192,128]{1,0:T(8,128)}, f32[128,8192]{1,0:T(8,128)}, bf16[8,8192]{1,0:T(8,128)(2,1)S(1)}) conditional(s32[]{:T(128)} %convert_element_type.119, (f32[8192,128]{1,0:T(8,128)}, f32[128,8192]{1,0:T(8,128)}) %tuple.66, (s32[2,12]{1,0:T(2,128)S(1)}, s32[]{:T(128)}, bf16[1,12,8,8192]{3,2,1,0:T(8,128)(2,1)}, pred[]{:T(512)}, ...), branch_computations={%region_1.1_spmd, %region_2.5_spmd} | conditional | flops 86523016 | bytes 102945120 | solution.py:102
  462.3 18.0 %conditional.7 = (f32[8192,128]{1,0:T(8,128)}, f32[128,8192]{1,0:T(8,128)}, bf16[8,8192]{1,0:T(8,128)(2,1)S(1)}) conditional(s32[]{:T(128)} %convert_element_type.120, (f32[8192,128]{1,0:T(8,128)}, f32[128,8192]{1,0:T(8,128)}) %tuple.68, (s32[2,12]{1,0:T(2,128)S(1)}, s32[]{:T(128)}, bf16[1,12,8,8192]{3,2,1,0:T(8,128)(2,1)}, pred[]{:T(512)}, ...), branch_computations={%region_6.6_spmd, %region_7.10_spmd} | conditional | flops 86523016 | bytes 102945120 | solution.py:102
  484.2 6.5 collective-permute-done.1
  490.7 16.6 %conditional.6 = (f32[8192,128]{1,0:T(8,128)}, f32[128,8192]{1,0:T(8,128)}, bf16[8,8192]{1,0:T(8,128)(2,1)S(1)}) conditional(s32[]{:T(128)} %convert_element_type.119, (f32[8192,128]{1,0:T(8,128)}, f32[128,8192]{1,0:T(8,128)}) %tuple.66, (s32[2,12]{1,0:T(2,128)S(1)}, s32[]{:T(128)}, bf16[1,12,8,8192]{3,2,1,0:T(8,128)(2,1)}, pred[]{:T(512)}, ...), branch_computations={%region_1.1_spmd, %region_2.5_spmd} | conditional | flops 86523016 | bytes 102945120 | solution.py:102
  509.2 18.0 %conditional.7 = (f32[8192,128]{1,0:T(8,128)}, f32[128,8192]{1,0:T(8,128)}, bf16[8,8192]{1,0:T(8,128)(2,1)S(1)}) conditional(s32[]{:T(128)} %convert_element_type.120, (f32[8192,128]{1,0:T(8,128)}, f32[128,8192]{1,0:T(8,128)}) %tuple.68, (s32[2,12]{1,0:T(2,128)S(1)}, s32[]{:T(128)}, bf16[1,12,8,8192]{3,2,1,0:T(8,128)(2,1)}, pred[]{:T(512)}, ...), branch_computations={%region_6.6_spmd, %region_7.10_spmd} | conditional | flops 86523016 | bytes 102945120 | solution.py:102
  531.1 6.5 collective-permute-done.1
  537.7 16.6 %conditional.6 = (f32[8192,128]{1,0:T(8,128)}, f32[128,8192]{1,0:T(8,128)}, bf16[8,8192]{1,0:T(8,128)(2,1)S(1)}) conditional(s32[]{:T(128)} %convert_element_type.119, (f32[8192,128]{1,0:T(8,128)}, f32[128,8192]{1,0:T(8,128)}) %tuple.66, (s32[2,12]{1,0:T(2,128)S(1)}, s32[]{:T(128)}, bf16[1,12,8,8192]{3,2,1,0:T(8,128)(2,1)}, pred[]{:T(512)}, ...), branch_computations={%region_1.1_spmd, %region_2.5_spmd} | conditional | flops 86523016 | bytes 102945120 | solution.py:102
  556.2 18.0 %conditional.7 = (f32[8192,128]{1,0:T(8,128)}, f32[128,8192]{1,0:T(8,128)}, bf16[8,8192]{1,0:T(8,128)(2,1)S(1)}) conditional(s32[]{:T(128)} %convert_element_type.120, (f32[8192,128]{1,0:T(8,128)}, f32[128,8192]{1,0:T(8,128)}) %tuple.68, (s32[2,12]{1,0:T(2,128)S(1)}, s32[]{:T(128)}, bf16[1,12,8,8192]{3,2,1,0:T(8,128)(2,1)}, pred[]{:T(512)}, ...), branch_computations={%region_6.6_spmd, %region_7.10_spmd} | conditional | flops 86523016 | bytes 102945120 | solution.py:102
  578.1 6.5 collective-permute-done.1
  584.6 16.6 %conditional.6 = (f32[8192,128]{1,0:T(8,128)}, f32[128,8192]{1,0:T(8,128)}, bf16[8,8192]{1,0:T(8,128)(2,1)S(1)}) conditional(s32[]{:T(128)} %convert_element_type.119, (f32[8192,128]{1,0:T(8,128)}, f32[128,8192]{1,0:T(8,128)}) %tuple.66, (s32[2,12]{1,0:T(2,128)S(1)}, s32[]{:T(128)}, bf16[1,12,8,8192]{3,2,1,0:T(8,128)(2,1)}, pred[]{:T(512)}, ...), branch_computations={%region_1.1_spmd, %region_2.5_spmd} | conditional | flops 86523016 | bytes 102945120 | solution.py:102
  603.1 18.0 %conditional.7 = (f32[8192,128]{1,0:T(8,128)}, f32[128,8192]{1,0:T(8,128)}, bf16[8,8192]{1,0:T(8,128)(2,1)S(1)}) conditional(s32[]{:T(128)} %convert_element_type.120, (f32[8192,128]{1,0:T(8,128)}, f32[128,8192]{1,0:T(8,128)}) %tuple.68, (s32[2,12]{1,0:T(2,128)S(1)}, s32[]{:T(128)}, bf16[1,12,8,8192]{3,2,1,0:T(8,128)(2,1)}, pred[]{:T(512)}, ...), branch_computations={%region_6.6_spmd, %region_7.10_spmd} | conditional | flops 86523016 | bytes 102945120 | solution.py:102
  625.1 6.5 collective-permute-done.1
  631.6 16.6 %conditional.6 = (f32[8192,128]{1,0:T(8,128)}, f32[128,8192]{1,0:T(8,128)}, bf16[8,8192]{1,0:T(8,128)(2,1)S(1)}) conditional(s32[]{:T(128)} %convert_element_type.119, (f32[8192,128]{1,0:T(8,128)}, f32[128,8192]{1,0:T(8,128)}) %tuple.66, (s32[2,12]{1,0:T(2,128)S(1)}, s32[]{:T(128)}, bf16[1,12,8,8192]{3,2,1,0:T(8,128)(2,1)}, pred[]{:T(512)}, ...), branch_computations={%region_1.1_spmd, %region_2.5_spmd} | conditional | flops 86523016 | bytes 102945120 | solution.py:102
  650.1 18.0 %conditional.7 = (f32[8192,128]{1,0:T(8,128)}, f32[128,8192]{1,0:T(8,128)}, bf16[8,8192]{1,0:T(8,128)(2,1)S(1)}) conditional(s32[]{:T(128)} %convert_element_type.120, (f32[8192,128]{1,0:T(8,128)}, f32[128,8192]{1,0:T(8,128)}) %tuple.68, (s32[2,12]{1,0:T(2,128)S(1)}, s32[]{:T(128)}, bf16[1,12,8,8192]{3,2,1,0:T(8,128)(2,1)}, pred[]{:T(512)}, ...), branch_computations={%region_6.6_spmd, %region_7.10_spmd} | conditional | flops 86523016 | bytes 102945120 | solution.py:102
  672.0 6.5 collective-permute-done.1
  678.6 16.6 %conditional.6 = (f32[8192,128]{1,0:T(8,128)}, f32[128,8192]{1,0:T(8,128)}, bf16[8,8192]{1,0:T(8,128)(2,1)S(1)}) conditional(s32[]{:T(128)} %convert_element_type.119, (f32[8192,128]{1,0:T(8,128)}, f32[128,8192]{1,0:T(8,128)}) %tuple.66, (s32[2,12]{1,0:T(2,128)S(1)}, s32[]{:T(128)}, bf16[1,12,8,8192]{3,2,1,0:T(8,128)(2,1)}, pred[]{:T(512)}, ...), branch_computations={%region_1.1_spmd, %region_2.5_spmd} | conditional | flops 86523016 | bytes 102945120 | solution.py:102
  697.1 18.0 %conditional.7 = (f32[8192,128]{1,0:T(8,128)}, f32[128,8192]{1,0:T(8,128)}, bf16[8,8192]{1,0:T(8,128)(2,1)S(1)}) conditional(s32[]{:T(128)} %convert_element_type.120, (f32[8192,128]{1,0:T(8,128)}, f32[128,8192]{1,0:T(8,128)}) %tuple.68, (s32[2,12]{1,0:T(2,128)S(1)}, s32[]{:T(128)}, bf16[1,12,8,8192]{3,2,1,0:T(8,128)(2,1)}, pred[]{:T(512)}, ...), branch_computations={%region_6.6_spmd, %region_7.10_spmd} | conditional | flops 86523016 | bytes 102945120 | solution.py:102
  719.0 6.5 collective-permute-done.1
  725.5 16.6 %conditional.6 = (f32[8192,128]{1,0:T(8,128)}, f32[128,8192]{1,0:T(8,128)}, bf16[8,8192]{1,0:T(8,128)(2,1)S(1)}) conditional(s32[]{:T(128)} %convert_element_type.119, (f32[8192,128]{1,0:T(8,128)}, f32[128,8192]{1,0:T(8,128)}) %tuple.66, (s32[2,12]{1,0:T(2,128)S(1)}, s32[]{:T(128)}, bf16[1,12,8,8192]{3,2,1,0:T(8,128)(2,1)}, pred[]{:T(512)}, ...), branch_computations={%region_1.1_spmd, %region_2.5_spmd} | conditional | flops 86523016 | bytes 102945120 | solution.py:102
  744.0 18.0 %conditional.7 = (f32[8192,128]{1,0:T(8,128)}, f32[128,8192]{1,0:T(8,128)}, bf16[8,8192]{1,0:T(8,128)(2,1)S(1)}) conditional(s32[]{:T(128)} %convert_element_type.120, (f32[8192,128]{1,0:T(8,128)}, f32[128,8192]{1,0:T(8,128)}) %tuple.68, (s32[2,12]{1,0:T(2,128)S(1)}, s32[]{:T(128)}, bf16[1,12,8,8192]{3,2,1,0:T(8,128)(2,1)}, pred[]{:T(512)}, ...), branch_computations={%region_6.6_spmd, %region_7.10_spmd} | conditional | flops 86523016 | bytes 102945120 | solution.py:102
  766.0 6.5 collective-permute-done.1
  772.5 16.6 %conditional.6 = (f32[8192,128]{1,0:T(8,128)}, f32[128,8192]{1,0:T(8,128)}, bf16[8,8192]{1,0:T(8,128)(2,1)S(1)}) conditional(s32[]{:T(128)} %convert_element_type.119, (f32[8192,128]{1,0:T(8,128)}, f32[128,8192]{1,0:T(8,128)}) %tuple.66, (s32[2,12]{1,0:T(2,128)S(1)}, s32[]{:T(128)}, bf16[1,12,8,8192]{3,2,1,0:T(8,128)(2,1)}, pred[]{:T(512)}, ...), branch_computations={%region_1.1_spmd, %region_2.5_spmd} | conditional | flops 86523016 | bytes 102945120 | solution.py:102
  791.0 18.0 %conditional.7 = (f32[8192,128]{1,0:T(8,128)}, f32[128,8192]{1,0:T(8,128)}, bf16[8,8192]{1,0:T(8,128)(2,1)S(1)}) conditional(s32[]{:T(128)} %convert_element_type.120, (f32[8192,128]{1,0:T(8,128)}, f32[128,8192]{1,0:T(8,128)}) %tuple.68, (s32[2,12]{1,0:T(2,128)S(1)}, s32[]{:T(128)}, bf16[1,12,8,8192]{3,2,1,0:T(8,128)(2,1)}, pred[]{:T(512)}, ...), branch_computations={%region_6.6_spmd, %region_7.10_spmd} | conditional | flops 86523016 | bytes 102945120 | solution.py:102
  812.9 6.5 collective-permute-done.1
  819.5 16.6 %conditional.6 = (f32[8192,128]{1,0:T(8,128)}, f32[128,8192]{1,0:T(8,128)}, bf16[8,8192]{1,0:T(8,128)(2,1)S(1)}) conditional(s32[]{:T(128)} %convert_element_type.119, (f32[8192,128]{1,0:T(8,128)}, f32[128,8192]{1,0:T(8,128)}) %tuple.66, (s32[2,12]{1,0:T(2,128)S(1)}, s32[]{:T(128)}, bf16[1,12,8,8192]{3,2,1,0:T(8,128)(2,1)}, pred[]{:T(512)}, ...), branch_computations={%region_1.1_spmd, %region_2.5_spmd} | conditional | flops 86523016 | bytes 102945120 | solution.py:102
  838.0 18.0 %conditional.7 = (f32[8192,128]{1,0:T(8,128)}, f32[128,8192]{1,0:T(8,128)}, bf16[8,8192]{1,0:T(8,128)(2,1)S(1)}) conditional(s32[]{:T(128)} %convert_element_type.120, (f32[8192,128]{1,0:T(8,128)}, f32[128,8192]{1,0:T(8,128)}) %tuple.68, (s32[2,12]{1,0:T(2,128)S(1)}, s32[]{:T(128)}, bf16[1,12,8,8192]{3,2,1,0:T(8,128)(2,1)}, pred[]{:T(512)}, ...), branch_computations={%region_6.6_spmd, %region_7.10_spmd} | conditional | flops 86523016 | bytes 102945120 | solution.py:102
  859.9 6.5 collective-permute-done.1
  866.4 16.6 %conditional.6 = (f32[8192,128]{1,0:T(8,128)}, f32[128,8192]{1,0:T(8,128)}, bf16[8,8192]{1,0:T(8,128)(2,1)S(1)}) conditional(s32[]{:T(128)} %convert_element_type.119, (f32[8192,128]{1,0:T(8,128)}, f32[128,8192]{1,0:T(8,128)}) %tuple.66, (s32[2,12]{1,0:T(2,128)S(1)}, s32[]{:T(128)}, bf16[1,12,8,8192]{3,2,1,0:T(8,128)(2,1)}, pred[]{:T(512)}, ...), branch_computations={%region_1.1_spmd, %region_2.5_spmd} | conditional | flops 86523016 | bytes 102945120 | solution.py:102
  884.9 18.0 %conditional.7 = (f32[8192,128]{1,0:T(8,128)}, f32[128,8192]{1,0:T(8,128)}, bf16[8,8192]{1,0:T(8,128)(2,1)S(1)}) conditional(s32[]{:T(128)} %convert_element_type.120, (f32[8192,128]{1,0:T(8,128)}, f32[128,8192]{1,0:T(8,128)}) %tuple.68, (s32[2,12]{1,0:T(2,128)S(1)}, s32[]{:T(128)}, bf16[1,12,8,8192]{3,2,1,0:T(8,128)(2,1)}, pred[]{:T(512)}, ...), branch_computations={%region_6.6_spmd, %region_7.10_spmd} | conditional | flops 86523016 | bytes 102945120 | solution.py:102
  906.9 6.5 collective-permute-done.1
  913.4 18.0 %collective-permute-start = (bf16[8,8192]{1,0:T(8,128)(2,1)S(1)}, bf16[8,8192]{1,0:T(8,128)(2,1)S(1)}, u32[]{:S(2)}, u32[]{:S(2)}) collective-permute-start(bf16[8,8192]{1,0:T(8,128)(2,1)S(1)} %get-tuple-element.853), channel_id=1, source_target_pairs={{16,0},{32,16},{48,32},{64,48},{80,64},{96,80},{112,96},{128,112},... | collective-permute-start | bytes 393224 | tf_op jit(solution)/shard_map/while/body/eval_jaxpr/ppermute | solution.py:16
  931.5 18.0 %conditional.7 = (f32[8192,128]{1,0:T(8,128)}, f32[128,8192]{1,0:T(8,128)}, bf16[8,8192]{1,0:T(8,128)(2,1)S(1)}) conditional(s32[]{:T(128)} %convert_element_type.120, (f32[8192,128]{1,0:T(8,128)}, f32[128,8192]{1,0:T(8,128)}) %tuple.68, (s32[2,12]{1,0:T(2,128)S(1)}, s32[]{:T(128)}, bf16[1,12,8,8192]{3,2,1,0:T(8,128)(2,1)}, pred[]{:T(512)}, ...), branch_computations={%region_6.6_spmd, %region_7.10_spmd} | conditional | flops 86523016 | bytes 102945120 | solution.py:102
  951.4 8.5 collective-permute-done.1
  961.9 21.9 %collective-permute-start.1 = (bf16[8,8192]{1,0:T(8,128)(2,1)S(1)}, bf16[8,8192]{1,0:T(8,128)(2,1)S(1)}, u32[]{:S(2)}, u32[]{:S(2)}) collective-permute-start(bf16[8,8192]{1,0:T(8,128)(2,1)S(1)} %get-tuple-element.854), channel_id=1, source_target_pairs={{0,16},{16,32},{32,48},{48,64},{64,80},{80,96},{96,112},{112,128},... | collective-permute-start | bytes 393224 | tf_op jit(solution)/shard_map/while/body/eval_jaxpr/ppermute | solution.py:16
  1000.8 18.2 %collective-permute-start.1 = (bf16[8,8192]{1,0:T(8,128)(2,1)S(1)}, bf16[8,8192]{1,0:T(8,128)(2,1)S(1)}, u32[]{:S(2)}, u32[]{:S(2)}) collective-permute-start(bf16[8,8192]{1,0:T(8,128)(2,1)S(1)} %get-tuple-element.854), channel_id=1, source_target_pairs={{0,16},{16,32},{32,48},{48,64},{64,80},{80,96},{96,112},{112,128},... | collective-permute-start | bytes 393224 | tf_op jit(solution)/shard_map/while/body/eval_jaxpr/ppermute | solution.py:16
  1036.1 18.2 %collective-permute-start.1 = (bf16[8,8192]{1,0:T(8,128)(2,1)S(1)}, bf16[8,8192]{1,0:T(8,128)(2,1)S(1)}, u32[]{:S(2)}, u32[]{:S(2)}) collective-permute-start(bf16[8,8192]{1,0:T(8,128)(2,1)S(1)} %get-tuple-element.854), channel_id=1, source_target_pairs={{0,16},{16,32},{32,48},{48,64},{64,80},{80,96},{96,112},{112,128},... | collective-permute-start | bytes 393224 | tf_op jit(solution)/shard_map/while/body/eval_jaxpr/ppermute | solution.py:16
  1071.4 20.0 %collective-permute-start.1 = (bf16[8,8192]{1,0:T(8,128)(2,1)S(1)}, bf16[8,8192]{1,0:T(8,128)(2,1)S(1)}, u32[]{:S(2)}, u32[]{:S(2)}) collective-permute-start(bf16[8,8192]{1,0:T(8,128)(2,1)S(1)} %get-tuple-element.854), channel_id=1, source_target_pairs={{0,16},{16,32},{32,48},{48,64},{64,80},{80,96},{96,112},{112,128},... | collective-permute-start | bytes 393224 | tf_op jit(solution)/shard_map/while/body/eval_jaxpr/ppermute | solution.py:16
  1109.2 115.3 %reduce-scatter.7.cloned.1.call-done = bf16[512,128]{1,0:T(8,128)(2,1)} async-done(((bf16[8192,128]{1,0:T(8,128)(2,1)}), bf16[512,128]{1,0:T(8,128)(2,1)}) %reduce-scatter.7.cloned.1.call-update) | async-done | bytes 131088 | tf_op jit(solution)/shard_map/reduce_scatter | solution.py:197
  1225.5 67.2 %reduce-scatter.9.cloned.1.call-done = bf16[128,512]{1,0:T(8,128)(2,1)} async-done(((bf16[128,8192]{1,0:T(8,128)(2,1)}), bf16[128,512]{1,0:T(8,128)(2,1)}) %reduce-scatter.9.cloned.1.call-update) | async-done | bytes 131088 | tf_op jit(solution)/shard_map/reduce_scatter | solution.py:200
  1295.2 7.3 collective-permute-done.6
  1304.6 13.1 collective-permute-done.7
  1322.4 8.3 collective-permute-done.8
  1331.2 8.8 collective-permute-done.9
  1340.1 21.4 %reduce-scatter.11.cloned.1.call-done = bf16[128,512]{1,0:T(8,128)(2,1)} async-done(((bf16[128,8192]{1,0:T(8,128)(2,1)}), bf16[128,512]{1,0:T(8,128)(2,1)}) %reduce-scatter.11.cloned.1.call-update) | async-done | bytes 131088 | tf_op jit(solution)/shard_map/reduce_scatter | solution.py:194
  1363.2 66.5 %reduce-scatter.5.cloned.1.call-done = bf16[512,128]{1,0:T(8,128)(2,1)} async-done(((bf16[8192,128]{1,0:T(8,128)(2,1)}), bf16[512,128]{1,0:T(8,128)(2,1)}) %reduce-scatter.5.cloned.1.call-update) | async-done | bytes 131088 | tf_op jit(solution)/shard_map/reduce_scatter | solution.py:191
  (805 shorter events, 610.7 us)
Async XLA Ops:
  7.2 54.4 %all-gather.12.cloned.1.call-start = ((), (), s32[]{:S(2)}) async-start(), calls=%async_computation.10 | async-start | bytes 2228224 | tf_op jit(solution)/shard_map/all_gather | solution.py:132
  7.9 78.9 %all-gather.10.cloned.1.call-start = ((), (), s32[]{:S(2)}) async-start(), calls=%async_computation.9 | async-start | bytes 2228224 | tf_op jit(solution)/shard_map/all_gather | solution.py:133
  8.7 117.0 %all-gather.8.cloned.1.call-start = ((), (), s32[]{:S(2)}) async-start(), calls=%async_computation.4 | async-start | bytes 2228224 | tf_op jit(solution)/shard_map/all_gather | solution.py:136
  10.6 8.3 collective-permute-start.2
  19.0 14.5 %collective-permute-start.3 = (bf16[2,128,512]{2,1,0:T(8,128)(2,1)S(1)}, bf16[2,128,512]{2,1,0:T(8,128)(2,1)S(1)}, u32[]{:S(2)}, u32[]{:S(2)}) collective-permute-start(bf16[2,128,512]{2,1,0:T(8,128)(2,1)S(1)} %collective-permute-done.2), channel_id=1, source_target_pairs={{0,32},{16,48},{32,0},{48,16},{64,96},{80,112},{96,64},{112,80},{1... | collective-permute-start | bytes 786440 | tf_op jit(solution)/shard_map/ppermute | solution.py:10
  33.5 17.9 %collective-permute-start.4 = (bf16[2,128,512]{2,1,0:T(8,128)(2,1)S(1)}, bf16[2,128,512]{2,1,0:T(8,128)(2,1)S(1)}, u32[]{:S(2)}, u32[]{:S(2)}) collective-permute-start(bf16[2,128,512]{2,1,0:T(8,128)(2,1)S(1)} %collective-permute-done.3), channel_id=1, source_target_pairs={{0,64},{16,80},{32,96},{48,112},{64,0},{80,16},{96,32},{112,48},{1... | collective-permute-start | bytes 786440 | tf_op jit(solution)/shard_map/ppermute | solution.py:10
  51.4 7.9 collective-permute-start.5
  60.7 103.6 %all-gather.14.cloned.1.call-start = ((), (), s32[]{:S(2)}) async-start(), calls=%async_computation.11 | async-start | bytes 2228224 | tf_op jit(solution)/shard_map/all_gather | solution.py:137
  61.3 1163.2 %reduce-scatter.7.cloned.1.call-start = ((), (), s32[]{:S(2)}) async-start(), calls=%async_computation.6 | async-start | bytes 2228224 | tf_op jit(solution)/shard_map/reduce_scatter | solution.py:197
  174.0 8.5 collective-permute-start
  179.4 10.9 collective-permute-start.1
  192.3 10.5 collective-permute-start.1
  204.8 10.5 collective-permute-start.1
  217.3 10.5 collective-permute-start.1
  230.5 23.1 %collective-permute-start.1 = (bf16[8,8192]{1,0:T(8,128)(2,1)S(1)}, bf16[8,8192]{1,0:T(8,128)(2,1)S(1)}, u32[]{:S(2)}, u32[]{:S(2)}) collective-permute-start(bf16[8,8192]{1,0:T(8,128)(2,1)S(1)} %get-tuple-element.854), channel_id=1, source_target_pairs={{0,16},{16,32},{32,48},{48,64},{64,80},{80,96},{96,112},{112,128},... | collective-permute-start | bytes 393224 | tf_op jit(solution)/shard_map/while/body/eval_jaxpr/ppermute | solution.py:16
  253.7 24.1 %collective-permute-start = (bf16[8,8192]{1,0:T(8,128)(2,1)S(1)}, bf16[8,8192]{1,0:T(8,128)(2,1)S(1)}, u32[]{:S(2)}, u32[]{:S(2)}) collective-permute-start(bf16[8,8192]{1,0:T(8,128)(2,1)S(1)} %get-tuple-element.853), channel_id=1, source_target_pairs={{16,0},{32,16},{48,32},{64,48},{80,64},{96,80},{112,96},{128,112},... | collective-permute-start | bytes 393224 | tf_op jit(solution)/shard_map/while/body/eval_jaxpr/ppermute | solution.py:16
  275.3 24.8 %collective-permute-start.1 = (bf16[8,8192]{1,0:T(8,128)(2,1)S(1)}, bf16[8,8192]{1,0:T(8,128)(2,1)S(1)}, u32[]{:S(2)}, u32[]{:S(2)}) collective-permute-start(bf16[8,8192]{1,0:T(8,128)(2,1)S(1)} %get-tuple-element.854), channel_id=1, source_target_pairs={{0,16},{16,32},{32,48},{48,64},{64,80},{80,96},{96,112},{112,128},... | collective-permute-start | bytes 393224 | tf_op jit(solution)/shard_map/while/body/eval_jaxpr/ppermute | solution.py:16
  300.1 42.5 %collective-permute-start = (bf16[8,8192]{1,0:T(8,128)(2,1)S(1)}, bf16[8,8192]{1,0:T(8,128)(2,1)S(1)}, u32[]{:S(2)}, u32[]{:S(2)}) collective-permute-start(bf16[8,8192]{1,0:T(8,128)(2,1)S(1)} %get-tuple-element.853), channel_id=1, source_target_pairs={{16,0},{32,16},{48,32},{64,48},{80,64},{96,80},{112,96},{128,112},... | collective-permute-start | bytes 393224 | tf_op jit(solution)/shard_map/while/body/eval_jaxpr/ppermute | solution.py:16
  322.0 26.0 %collective-permute-start.1 = (bf16[8,8192]{1,0:T(8,128)(2,1)S(1)}, bf16[8,8192]{1,0:T(8,128)(2,1)S(1)}, u32[]{:S(2)}, u32[]{:S(2)}) collective-permute-start(bf16[8,8192]{1,0:T(8,128)(2,1)S(1)} %get-tuple-element.854), channel_id=1, source_target_pairs={{0,16},{16,32},{32,48},{48,64},{64,80},{80,96},{96,112},{112,128},... | collective-permute-start | bytes 393224 | tf_op jit(solution)/shard_map/while/body/eval_jaxpr/ppermute | solution.py:16
  364.6 7.8 collective-permute-start
  370.0 24.8 %collective-permute-start.1 = (bf16[8,8192]{1,0:T(8,128)(2,1)S(1)}, bf16[8,8192]{1,0:T(8,128)(2,1)S(1)}, u32[]{:S(2)}, u32[]{:S(2)}) collective-permute-start(bf16[8,8192]{1,0:T(8,128)(2,1)S(1)} %get-tuple-element.854), channel_id=1, source_target_pairs={{0,16},{16,32},{32,48},{48,64},{64,80},{80,96},{96,112},{112,128},... | collective-permute-start | bytes 393224 | tf_op jit(solution)/shard_map/while/body/eval_jaxpr/ppermute | solution.py:16
  411.4 23.8 %collective-permute-start = (bf16[8,8192]{1,0:T(8,128)(2,1)S(1)}, bf16[8,8192]{1,0:T(8,128)(2,1)S(1)}, u32[]{:S(2)}, u32[]{:S(2)}) collective-permute-start(bf16[8,8192]{1,0:T(8,128)(2,1)S(1)} %get-tuple-element.853), channel_id=1, source_target_pairs={{16,0},{32,16},{48,32},{64,48},{80,64},{96,80},{112,96},{128,112},... | collective-permute-start | bytes 393224 | tf_op jit(solution)/shard_map/while/body/eval_jaxpr/ppermute | solution.py:16
  433.3 10.5 collective-permute-start.1
  460.3 23.8 %collective-permute-start = (bf16[8,8192]{1,0:T(8,128)(2,1)S(1)}, bf16[8,8192]{1,0:T(8,128)(2,1)S(1)}, u32[]{:S(2)}, u32[]{:S(2)}) collective-permute-start(bf16[8,8192]{1,0:T(8,128)(2,1)S(1)} %get-tuple-element.853), channel_id=1, source_target_pairs={{16,0},{32,16},{48,32},{64,48},{80,64},{96,80},{112,96},{128,112},... | collective-permute-start | bytes 393224 | tf_op jit(solution)/shard_map/while/body/eval_jaxpr/ppermute | solution.py:16
  480.2 10.5 collective-permute-start.1
  507.3 23.8 %collective-permute-start = (bf16[8,8192]{1,0:T(8,128)(2,1)S(1)}, bf16[8,8192]{1,0:T(8,128)(2,1)S(1)}, u32[]{:S(2)}, u32[]{:S(2)}) collective-permute-start(bf16[8,8192]{1,0:T(8,128)(2,1)S(1)} %get-tuple-element.853), channel_id=1, source_target_pairs={{16,0},{32,16},{48,32},{64,48},{80,64},{96,80},{112,96},{128,112},... | collective-permute-start | bytes 393224 | tf_op jit(solution)/shard_map/while/body/eval_jaxpr/ppermute | solution.py:16
  527.2 10.5 collective-permute-start.1
  554.3 23.8 %collective-permute-start = (bf16[8,8192]{1,0:T(8,128)(2,1)S(1)}, bf16[8,8192]{1,0:T(8,128)(2,1)S(1)}, u32[]{:S(2)}, u32[]{:S(2)}) collective-permute-start(bf16[8,8192]{1,0:T(8,128)(2,1)S(1)} %get-tuple-element.853), channel_id=1, source_target_pairs={{16,0},{32,16},{48,32},{64,48},{80,64},{96,80},{112,96},{128,112},... | collective-permute-start | bytes 393224 | tf_op jit(solution)/shard_map/while/body/eval_jaxpr/ppermute | solution.py:16
  574.2 10.5 collective-permute-start.1
  601.2 23.8 %collective-permute-start = (bf16[8,8192]{1,0:T(8,128)(2,1)S(1)}, bf16[8,8192]{1,0:T(8,128)(2,1)S(1)}, u32[]{:S(2)}, u32[]{:S(2)}) collective-permute-start(bf16[8,8192]{1,0:T(8,128)(2,1)S(1)} %get-tuple-element.853), channel_id=1, source_target_pairs={{16,0},{32,16},{48,32},{64,48},{80,64},{96,80},{112,96},{128,112},... | collective-permute-start | bytes 393224 | tf_op jit(solution)/shard_map/while/body/eval_jaxpr/ppermute | solution.py:16
  621.1 10.5 collective-permute-start.1
  648.2 23.8 %collective-permute-start = (bf16[8,8192]{1,0:T(8,128)(2,1)S(1)}, bf16[8,8192]{1,0:T(8,128)(2,1)S(1)}, u32[]{:S(2)}, u32[]{:S(2)}) collective-permute-start(bf16[8,8192]{1,0:T(8,128)(2,1)S(1)} %get-tuple-element.853), channel_id=1, source_target_pairs={{16,0},{32,16},{48,32},{64,48},{80,64},{96,80},{112,96},{128,112},... | collective-permute-start | bytes 393224 | tf_op jit(solution)/shard_map/while/body/eval_jaxpr/ppermute | solution.py:16
  668.1 10.5 collective-permute-start.1
  695.2 23.8 %collective-permute-start = (bf16[8,8192]{1,0:T(8,128)(2,1)S(1)}, bf16[8,8192]{1,0:T(8,128)(2,1)S(1)}, u32[]{:S(2)}, u32[]{:S(2)}) collective-permute-start(bf16[8,8192]{1,0:T(8,128)(2,1)S(1)} %get-tuple-element.853), channel_id=1, source_target_pairs={{16,0},{32,16},{48,32},{64,48},{80,64},{96,80},{112,96},{128,112},... | collective-permute-start | bytes 393224 | tf_op jit(solution)/shard_map/while/body/eval_jaxpr/ppermute | solution.py:16
  715.1 10.5 collective-permute-start.1
  742.1 23.8 %collective-permute-start = (bf16[8,8192]{1,0:T(8,128)(2,1)S(1)}, bf16[8,8192]{1,0:T(8,128)(2,1)S(1)}, u32[]{:S(2)}, u32[]{:S(2)}) collective-permute-start(bf16[8,8192]{1,0:T(8,128)(2,1)S(1)} %get-tuple-element.853), channel_id=1, source_target_pairs={{16,0},{32,16},{48,32},{64,48},{80,64},{96,80},{112,96},{128,112},... | collective-permute-start | bytes 393224 | tf_op jit(solution)/shard_map/while/body/eval_jaxpr/ppermute | solution.py:16
  762.0 10.5 collective-permute-start.1
  789.1 23.8 %collective-permute-start = (bf16[8,8192]{1,0:T(8,128)(2,1)S(1)}, bf16[8,8192]{1,0:T(8,128)(2,1)S(1)}, u32[]{:S(2)}, u32[]{:S(2)}) collective-permute-start(bf16[8,8192]{1,0:T(8,128)(2,1)S(1)} %get-tuple-element.853), channel_id=1, source_target_pairs={{16,0},{32,16},{48,32},{64,48},{80,64},{96,80},{112,96},{128,112},... | collective-permute-start | bytes 393224 | tf_op jit(solution)/shard_map/while/body/eval_jaxpr/ppermute | solution.py:16
  809.0 10.5 collective-permute-start.1
  836.0 23.8 %collective-permute-start = (bf16[8,8192]{1,0:T(8,128)(2,1)S(1)}, bf16[8,8192]{1,0:T(8,128)(2,1)S(1)}, u32[]{:S(2)}, u32[]{:S(2)}) collective-permute-start(bf16[8,8192]{1,0:T(8,128)(2,1)S(1)} %get-tuple-element.853), channel_id=1, source_target_pairs={{16,0},{32,16},{48,32},{64,48},{80,64},{96,80},{112,96},{128,112},... | collective-permute-start | bytes 393224 | tf_op jit(solution)/shard_map/while/body/eval_jaxpr/ppermute | solution.py:16
  856.0 10.5 collective-permute-start.1
  883.0 23.8 %collective-permute-start = (bf16[8,8192]{1,0:T(8,128)(2,1)S(1)}, bf16[8,8192]{1,0:T(8,128)(2,1)S(1)}, u32[]{:S(2)}, u32[]{:S(2)}) collective-permute-start(bf16[8,8192]{1,0:T(8,128)(2,1)S(1)} %get-tuple-element.853), channel_id=1, source_target_pairs={{16,0},{32,16},{48,32},{64,48},{80,64},{96,80},{112,96},{128,112},... | collective-permute-start | bytes 393224 | tf_op jit(solution)/shard_map/while/body/eval_jaxpr/ppermute | solution.py:16
  902.9 10.5 collective-permute-start.1
  913.4 38.0 %collective-permute-start = (bf16[8,8192]{1,0:T(8,128)(2,1)S(1)}, bf16[8,8192]{1,0:T(8,128)(2,1)S(1)}, u32[]{:S(2)}, u32[]{:S(2)}) collective-permute-start(bf16[8,8192]{1,0:T(8,128)(2,1)S(1)} %get-tuple-element.853), channel_id=1, source_target_pairs={{16,0},{32,16},{48,32},{64,48},{80,64},{96,80},{112,96},{128,112},... | collective-permute-start | bytes 393224 | tf_op jit(solution)/shard_map/while/body/eval_jaxpr/ppermute | solution.py:16
  949.5 10.5 collective-permute-start.1
  960.0 23.9 %collective-permute-start = (bf16[8,8192]{1,0:T(8,128)(2,1)S(1)}, bf16[8,8192]{1,0:T(8,128)(2,1)S(1)}, u32[]{:S(2)}, u32[]{:S(2)}) collective-permute-start(bf16[8,8192]{1,0:T(8,128)(2,1)S(1)} %get-tuple-element.853), channel_id=1, source_target_pairs={{16,0},{32,16},{48,32},{64,48},{80,64},{96,80},{112,96},{128,112},... | collective-permute-start | bytes 393224 | tf_op jit(solution)/shard_map/while/body/eval_jaxpr/ppermute | solution.py:16
  961.9 24.4 %collective-permute-start.1 = (bf16[8,8192]{1,0:T(8,128)(2,1)S(1)}, bf16[8,8192]{1,0:T(8,128)(2,1)S(1)}, u32[]{:S(2)}, u32[]{:S(2)}) collective-permute-start(bf16[8,8192]{1,0:T(8,128)(2,1)S(1)} %get-tuple-element.854), channel_id=1, source_target_pairs={{0,16},{16,32},{32,48},{48,64},{64,80},{80,96},{96,112},{112,128},... | collective-permute-start | bytes 393224 | tf_op jit(solution)/shard_map/while/body/eval_jaxpr/ppermute | solution.py:16
  986.3 8.0 collective-permute-start
  988.3 10.5 collective-permute-start.1
  998.8 21.2 %collective-permute-start = (bf16[8,8192]{1,0:T(8,128)(2,1)S(1)}, bf16[8,8192]{1,0:T(8,128)(2,1)S(1)}, u32[]{:S(2)}, u32[]{:S(2)}) collective-permute-start(bf16[8,8192]{1,0:T(8,128)(2,1)S(1)} %get-tuple-element.853), channel_id=1, source_target_pairs={{16,0},{32,16},{48,32},{64,48},{80,64},{96,80},{112,96},{128,112},... | collective-permute-start | bytes 393224 | tf_op jit(solution)/shard_map/while/body/eval_jaxpr/ppermute | solution.py:16
  1000.8 20.7 %collective-permute-start.1 = (bf16[8,8192]{1,0:T(8,128)(2,1)S(1)}, bf16[8,8192]{1,0:T(8,128)(2,1)S(1)}, u32[]{:S(2)}, u32[]{:S(2)}) collective-permute-start(bf16[8,8192]{1,0:T(8,128)(2,1)S(1)} %get-tuple-element.854), channel_id=1, source_target_pairs={{0,16},{16,32},{32,48},{48,64},{64,80},{80,96},{96,112},{112,128},... | collective-permute-start | bytes 393224 | tf_op jit(solution)/shard_map/while/body/eval_jaxpr/ppermute | solution.py:16
  1023.6 10.5 collective-permute-start.1
  1034.1 21.2 %collective-permute-start = (bf16[8,8192]{1,0:T(8,128)(2,1)S(1)}, bf16[8,8192]{1,0:T(8,128)(2,1)S(1)}, u32[]{:S(2)}, u32[]{:S(2)}) collective-permute-start(bf16[8,8192]{1,0:T(8,128)(2,1)S(1)} %get-tuple-element.853), channel_id=1, source_target_pairs={{16,0},{32,16},{48,32},{64,48},{80,64},{96,80},{112,96},{128,112},... | collective-permute-start | bytes 393224 | tf_op jit(solution)/shard_map/while/body/eval_jaxpr/ppermute | solution.py:16
  1036.1 20.7 %collective-permute-start.1 = (bf16[8,8192]{1,0:T(8,128)(2,1)S(1)}, bf16[8,8192]{1,0:T(8,128)(2,1)S(1)}, u32[]{:S(2)}, u32[]{:S(2)}) collective-permute-start(bf16[8,8192]{1,0:T(8,128)(2,1)S(1)} %get-tuple-element.854), channel_id=1, source_target_pairs={{0,16},{16,32},{32,48},{48,64},{64,80},{80,96},{96,112},{112,128},... | collective-permute-start | bytes 393224 | tf_op jit(solution)/shard_map/while/body/eval_jaxpr/ppermute | solution.py:16
  1058.9 10.5 collective-permute-start.1
  1069.4 23.0 %collective-permute-start = (bf16[8,8192]{1,0:T(8,128)(2,1)S(1)}, bf16[8,8192]{1,0:T(8,128)(2,1)S(1)}, u32[]{:S(2)}, u32[]{:S(2)}) collective-permute-start(bf16[8,8192]{1,0:T(8,128)(2,1)S(1)} %get-tuple-element.853), channel_id=1, source_target_pairs={{16,0},{32,16},{48,32},{64,48},{80,64},{96,80},{112,96},{128,112},... | collective-permute-start | bytes 393224 | tf_op jit(solution)/shard_map/while/body/eval_jaxpr/ppermute | solution.py:16
  1071.4 22.5 %collective-permute-start.1 = (bf16[8,8192]{1,0:T(8,128)(2,1)S(1)}, bf16[8,8192]{1,0:T(8,128)(2,1)S(1)}, u32[]{:S(2)}, u32[]{:S(2)}) collective-permute-start(bf16[8,8192]{1,0:T(8,128)(2,1)S(1)} %get-tuple-element.854), channel_id=1, source_target_pairs={{0,16},{16,32},{32,48},{48,64},{64,80},{80,96},{96,112},{112,128},... | collective-permute-start | bytes 393224 | tf_op jit(solution)/shard_map/while/body/eval_jaxpr/ppermute | solution.py:16
  1097.6 195.1 %reduce-scatter.9.cloned.1.call-start = ((), (), s32[]{:S(2)}) async-start(), calls=%async_computation.7 | async-start | bytes 2228224 | tf_op jit(solution)/shard_map/reduce_scatter | solution.py:200
  1101.5 260.0 %reduce-scatter.11.cloned.1.call-start = ((), (), s32[]{:S(2)}) async-start(), calls=%async_computation.8 | async-start | bytes 2228224 | tf_op jit(solution)/shard_map/reduce_scatter | solution.py:194
  1105.4 324.3 %reduce-scatter.5.cloned.1.call-start = ((), (), s32[]{:S(2)}) async-start(), calls=%async_computation.5 | async-start | bytes 2228224 | tf_op jit(solution)/shard_map/reduce_scatter | solution.py:191
  1293.7 8.8 collective-permute-start.6
  1302.5 15.2 %collective-permute-start.7 = (bf16[2,128,512]{2,1,0:T(8,128)(2,1)S(1)}, bf16[2,128,512]{2,1,0:T(8,128)(2,1)S(1)}, u32[]{:S(2)}, u32[]{:S(2)}) collective-permute-start(bf16[2,128,512]{2,1,0:T(8,128)(2,1)S(1)} %collective-permute-done.6), channel_id=1, source_target_pairs={{0,32},{16,48},{32,0},{48,16},{64,96},{80,112},{96,64},{112,80},{1... | collective-permute-start | bytes 786440 | tf_op jit(solution)/shard_map/ppermute | solution.py:10
  1317.7 13.1 collective-permute-start.8
  1330.7 9.3 collective-permute-start.9
  (131 other events, 495.3 us)
Sparse Core Ops, SparseCore 0:
  9.8 38.6 all-gather.11
  50.3 36.4 all-gather.9
  89.3 36.3 all-gather.7
  128.0 36.3 all-gather.13
  1097.8 126.7 reduce-scatter.6
  1226.9 65.8 reduce-scatter.8
  1295.3 66.2 reduce-scatter.10
  1364.1 65.5 reduce-scatter.4
where the time goes:
time: 1440 us
  waiting for transfers between devices  661 us (46%)
  starting transfers between devices  313 us (22%)
  matrix products  199 us (14%)
  local copies, waits for them, and re-layouts  149 us (10%)
  loops' own time  53.4 us (4%)
  other arithmetic  48.8 us (3%)
    ppermute x54, starting transfers between devices, passed_along(): lax.ppermute(value, axis, [(source, source + steps) for source in range(i...  292 us
    ppermute x54, waiting for transfers between devices, passed_along(): lax.ppermute(value, axis, [(source, source + steps) for source in range(i...  211 us
    reduce_scatter x1, waiting for transfers between devices, on_device(): lax.psum_scatter(state_up[0].astype(jnp.bfloat16), 'fsdp', scatter_dimens...  115 us
    cond x240, local copies, waits for them, and re-layouts  81.5 us
    ppermute x8, waiting for transfers between devices, from_partner(): return lax.ppermute(value, axis, pairs)  74.3 us
    dot_general x24, matrix products, active(): lax.dot_general(rows_in, grad_pre, (((0,), (0,)), ((), ())), preferred_el...  73.4 us
    reduce_scatter x1, waiting for transfers between devices, on_device(): lax.psum_scatter(state_up[1].astype(jnp.bfloat16), 'fsdp', scatter_dimens...  67.2 us
    reduce_scatter x1, waiting for transfers between devices, on_device(): lax.psum_scatter(state_down[0].astype(jnp.bfloat16), 'fsdp', scatter_dime...  66.5 us
  transfers between devices with their start and end apart: 70, of which 56 were waited for; matrix products, arithmetic and copies ran while one was open for 12% of the time, Pallas kernels for 0%

commit v1 on v0

--- a/solution.py
+++ b/solution.py
@@ -133,7 +133,15 @@
         lax.all_gather(own_out_shard, "fsdp", axis=1, tiled=True),
     )
     far_in, far_out = (
-        lax.all_gather(far_in_shard, "fsdp", axis=0, tiled=True),
+        jnp.concatenate(
+            lax.all_to_all(
+                jnp.stack([far_in_shard for _ in range(lax.psum(1, axis_name="fsdp"))]),
+                axis_name="fsdp",
+                split_axis=0,
+                concat_axis=0,
+            ),
+            axis=0,
+        ),
         lax.all_gather(far_out_shard, "fsdp", axis=1, tiled=True),
     )
     zero_in = jnp.zeros(own_in.shape, jnp.float32)

time: 1440 us -> 1380 us (0.958)
  waiting for transfers between devices: 661 us -> 600 us
    all_gather x1 -> x0, waiting for transfers between devices: 38.9 us -> none  [on_device(): lax.all_gather(far_in_shard, 'fsdp', axis=0, tiled=True)]
    all_to_all x0 -> x1, waiting for transfers between devices: none -> 31.7 us  [on_device(): lax.all_to_all(jnp.stack([far_in_shard for _ in range(lax.psum(1, axis_na...]
    ppermute x54, waiting for transfers between devices: 211 us -> 184 us  [passed_along(): lax.ppermute(value, axis, [(source, source + steps) for source in range(i...]
    all_gather x1, waiting for transfers between devices: 25.2 us -> 2.78 us  [on_device(): lax.all_gather(own_out_shard, 'fsdp', axis=1, tiled=True)]
  transfers between devices with their start and end apart: 70 -> 70, of which waited for: 56 -> 56; matrix products, arithmetic and copies ran while one was open for 12% -> 10% of each run, Pallas kernels for 0% -> 0%
where the time goes in v1:
time: 1380 us; the launch traced here: 1370 us
  waiting for transfers between devices  600 us (43%)
  starting transfers between devices  323 us (23%)
  matrix products  199 us (14%)
  local copies, waits for them, and re-layouts  148 us (11%)
  other arithmetic  45.8 us (3%)
  loops' own time  44.2 us (3%)
  between operations  14.2 us (1%)
    ppermute x54, starting transfers between devices, passed_along(): lax.ppermute(value, axis, [(source, source + steps) for source in range(i...  296 us
    ppermute x54, waiting for transfers between devices, passed_along(): lax.ppermute(value, axis, [(source, source + steps) for source in range(i...  184 us
    reduce_scatter x1, waiting for transfers between devices, on_device(): lax.psum_scatter(state_up[0].astype(jnp.bfloat16), 'fsdp', scatter_dimens...  110 us
    cond x240, local copies, waits for them, and re-layouts  81.6 us
    dot_general x24, matrix products, active(): lax.dot_general(rows_in, grad_pre, (((0,), (0,)), ((), ())), preferred_el...  73.4 us
    ppermute x8, waiting for transfers between devices, from_partner(): return lax.ppermute(value, axis, pairs)  73.2 us
    reduce_scatter x1, waiting for transfers between devices, on_device(): lax.psum_scatter(state_up[1].astype(jnp.bfloat16), 'fsdp', scatter_dimens...  66.8 us
    reduce_scatter x1, waiting for transfers between devices, on_device(): lax.psum_scatter(state_down[0].astype(jnp.bfloat16), 'fsdp', scatter_dime...  66.8 us
  transfers between devices with their start and end apart: 70, of which 56 were waited for; matrix products, arithmetic and copies ran while one was open for 10% of the time, Pallas kernels for 0%

profile of v1, /device:TPU:16, one launch (start us, length us, event | category | flops | bytes accessed | tf_op | source)
XLA Modules:
  0.0 1374.7 jit_solution(14848681605386206604)
XLA Ops:
  12.6 6.3 collective-permute-done.2
  22.2 11.2 collective-permute-done.3
  33.4 6.2 collective-permute-start.4
  39.7 11.7 collective-permute-done.4
  51.7 7.5 collective-permute-done.5
  67.4 31.7 %all-to-all-done = bf16[16,512,128]{2,1,0:T(8,128)(2,1)S(1)} async-done(((bf16[16,512,128]{2,1,0:T(8,128)(2,1)}), bf16[16,512,128]{2,1,0:T(8,128)(2,1)S(1)}, u32[]{:S(2)}, u32[]{:S(2)}) %all-to-all-start) | async-done | bytes 2097184 | tf_op jit(solution)/shard_map/all_to_all | solution.py:137
  101.8 42.2 %all-gather.11.cloned.1.call-done = bf16[1,128,8192]{2,1,0:T(8,128)(2,1)} async-done(((bf16[1,128,512]{2,1,0:T(8,128)(2,1)}), bf16[1,128,8192]{2,1,0:T(8,128)(2,1)}) %all-gather.11.cloned.1.call-update) | async-done | bytes 2097168 | tf_op jit(solution)/shard_map/all_gather | solution.py:145
  153.4 882.9 %while.25 = (s32[]{:T(128)}, bf16[8,8192]{1,0:T(8,128)(2,1)S(1)}, bf16[8,8192]{1,0:T(8,128)(2,1)S(1)}, f32[8192,128]{1,0:T(8,128)}, f32[128,8192]{1,0:T(8,128)},...) while((s32[]{:T(128)}, bf16[8,8192]{1,0:T(8,128)(2,1)S(1)}, ...), condition=%wide.region_11.12_spmd.clone, body=%wide.region_0.11_spmd.clone.sunk | while | flops 173046048 | bytes 206939488 | solution.py:193
  161.9 7.8 collective-permute-done.1
  176.6 5.6 collective-permute-done.1
  214.1 15.1 %collective-permute-done.1 = bf16[8,8192]{1,0:T(8,128)(2,1)S(1)} collective-permute-done((bf16[8,8192]{1,0:T(8,128)(2,1)S(1)}, bf16[8,8192]{1,0:T(8,128)(2,1)S(1)}, u32[]{:S(2)}, u32[]{:S(2)}) %collective-permute-start.1) | collective-permute-done | bytes 131104 | tf_op jit(solution)/shard_map/while/body/eval_jaxpr/ppermute | solution.py:16
  229.2 19.6 %collective-permute-start = (bf16[8,8192]{1,0:T(8,128)(2,1)S(1)}, bf16[8,8192]{1,0:T(8,128)(2,1)S(1)}, u32[]{:S(2)}, u32[]{:S(2)}) collective-permute-start(bf16[8,8192]{1,0:T(8,128)(2,1)S(1)} %get-tuple-element.853), channel_id=1, source_target_pairs={{16,0},{32,16},{48,32},{64,48},{80,64},{96,80},{112,96},{128,112},... | collective-permute-start | bytes 393224 | tf_op jit(solution)/shard_map/while/body/eval_jaxpr/ppermute | solution.py:16
  251.4 20.4 %collective-permute-done.1 = bf16[8,8192]{1,0:T(8,128)(2,1)S(1)} collective-permute-done((bf16[8,8192]{1,0:T(8,128)(2,1)S(1)}, bf16[8,8192]{1,0:T(8,128)(2,1)S(1)}, u32[]{:S(2)}, u32[]{:S(2)}) %collective-permute-start.1) | collective-permute-done | bytes 131104 | tf_op jit(solution)/shard_map/while/body/eval_jaxpr/ppermute | solution.py:16
  271.9 19.9 %collective-permute-start = (bf16[8,8192]{1,0:T(8,128)(2,1)S(1)}, bf16[8,8192]{1,0:T(8,128)(2,1)S(1)}, u32[]{:S(2)}, u32[]{:S(2)}) collective-permute-start(bf16[8,8192]{1,0:T(8,128)(2,1)S(1)} %get-tuple-element.853), channel_id=1, source_target_pairs={{16,0},{32,16},{48,32},{64,48},{80,64},{96,80},{112,96},{128,112},... | collective-permute-start | bytes 393224 | tf_op jit(solution)/shard_map/while/body/eval_jaxpr/ppermute | solution.py:16
  291.9 34.5 %collective-permute-start.1 = (bf16[8,8192]{1,0:T(8,128)(2,1)S(1)}, bf16[8,8192]{1,0:T(8,128)(2,1)S(1)}, u32[]{:S(2)}, u32[]{:S(2)}) collective-permute-start(bf16[8,8192]{1,0:T(8,128)(2,1)S(1)} %get-tuple-element.854), channel_id=1, source_target_pairs={{0,16},{16,32},{32,48},{48,64},{64,80},{80,96},{96,112},{112,128},... | collective-permute-start | bytes 393224 | tf_op jit(solution)/shard_map/while/body/eval_jaxpr/ppermute | solution.py:16
  328.9 17.3 %conditional.6 = (f32[8192,128]{1,0:T(8,128)}, f32[128,8192]{1,0:T(8,128)}, bf16[8,8192]{1,0:T(8,128)(2,1)S(1)}) conditional(s32[]{:T(128)} %convert_element_type.119, (f32[8192,128]{1,0:T(8,128)}, f32[128,8192]{1,0:T(8,128)}) %tuple.66, (s32[2,12]{1,0:T(2,128)S(1)}, s32[]{:T(128)}, bf16[1,12,8,8192]{3,2,1,0:T(8,128)(2,1)}, pred[]{:T(512)}, ...), branch_computations={%region_1.1_spmd, %region_2.5_spmd} | conditional | flops 86523016 | bytes 102945120 | solution.py:102
  358.8 17.3 %conditional.6 = (f32[8192,128]{1,0:T(8,128)}, f32[128,8192]{1,0:T(8,128)}, bf16[8,8192]{1,0:T(8,128)(2,1)S(1)}) conditional(s32[]{:T(128)} %convert_element_type.119, (f32[8192,128]{1,0:T(8,128)}, f32[128,8192]{1,0:T(8,128)}) %tuple.66, (s32[2,12]{1,0:T(2,128)S(1)}, s32[]{:T(128)}, bf16[1,12,8,8192]{3,2,1,0:T(8,128)(2,1)}, pred[]{:T(512)}, ...), branch_computations={%region_1.1_spmd, %region_2.5_spmd} | conditional | flops 86523016 | bytes 102945120 | solution.py:102
  380.1 16.1 %conditional.7 = (f32[8192,128]{1,0:T(8,128)}, f32[128,8192]{1,0:T(8,128)}, bf16[8,8192]{1,0:T(8,128)(2,1)S(1)}) conditional(s32[]{:T(128)} %convert_element_type.120, (f32[8192,128]{1,0:T(8,128)}, f32[128,8192]{1,0:T(8,128)}) %tuple.68, (s32[2,12]{1,0:T(2,128)S(1)}, s32[]{:T(128)}, bf16[1,12,8,8192]{3,2,1,0:T(8,128)(2,1)}, pred[]{:T(512)}, ...), branch_computations={%region_6.6_spmd, %region_7.10_spmd} | conditional | flops 86523016 | bytes 102945120 | solution.py:102
  398.1 8.5 collective-permute-done.1
  406.6 17.3 %conditional.6 = (f32[8192,128]{1,0:T(8,128)}, f32[128,8192]{1,0:T(8,128)}, bf16[8,8192]{1,0:T(8,128)(2,1)S(1)}) conditional(s32[]{:T(128)} %convert_element_type.119, (f32[8192,128]{1,0:T(8,128)}, f32[128,8192]{1,0:T(8,128)}) %tuple.66, (s32[2,12]{1,0:T(2,128)S(1)}, s32[]{:T(128)}, bf16[1,12,8,8192]{3,2,1,0:T(8,128)(2,1)}, pred[]{:T(512)}, ...), branch_computations={%region_1.1_spmd, %region_2.5_spmd} | conditional | flops 86523016 | bytes 102945120 | solution.py:102
  425.9 16.1 %conditional.7 = (f32[8192,128]{1,0:T(8,128)}, f32[128,8192]{1,0:T(8,128)}, bf16[8,8192]{1,0:T(8,128)(2,1)S(1)}) conditional(s32[]{:T(128)} %convert_element_type.120, (f32[8192,128]{1,0:T(8,128)}, f32[128,8192]{1,0:T(8,128)}) %tuple.68, (s32[2,12]{1,0:T(2,128)S(1)}, s32[]{:T(128)}, bf16[1,12,8,8192]{3,2,1,0:T(8,128)(2,1)}, pred[]{:T(512)}, ...), branch_computations={%region_6.6_spmd, %region_7.10_spmd} | conditional | flops 86523016 | bytes 102945120 | solution.py:102
  445.9 6.5 collective-permute-done.1
  452.4 17.3 %conditional.6 = (f32[8192,128]{1,0:T(8,128)}, f32[128,8192]{1,0:T(8,128)}, bf16[8,8192]{1,0:T(8,128)(2,1)S(1)}) conditional(s32[]{:T(128)} %convert_element_type.119, (f32[8192,128]{1,0:T(8,128)}, f32[128,8192]{1,0:T(8,128)}) %tuple.66, (s32[2,12]{1,0:T(2,128)S(1)}, s32[]{:T(128)}, bf16[1,12,8,8192]{3,2,1,0:T(8,128)(2,1)}, pred[]{:T(512)}, ...), branch_computations={%region_1.1_spmd, %region_2.5_spmd} | conditional | flops 86523016 | bytes 102945120 | solution.py:102
  471.7 16.1 %conditional.7 = (f32[8192,128]{1,0:T(8,128)}, f32[128,8192]{1,0:T(8,128)}, bf16[8,8192]{1,0:T(8,128)(2,1)S(1)}) conditional(s32[]{:T(128)} %convert_element_type.120, (f32[8192,128]{1,0:T(8,128)}, f32[128,8192]{1,0:T(8,128)}) %tuple.68, (s32[2,12]{1,0:T(2,128)S(1)}, s32[]{:T(128)}, bf16[1,12,8,8192]{3,2,1,0:T(8,128)(2,1)}, pred[]{:T(512)}, ...), branch_computations={%region_6.6_spmd, %region_7.10_spmd} | conditional | flops 86523016 | bytes 102945120 | solution.py:102
  491.7 6.5 collective-permute-done.1
  498.2 17.3 %conditional.6 = (f32[8192,128]{1,0:T(8,128)}, f32[128,8192]{1,0:T(8,128)}, bf16[8,8192]{1,0:T(8,128)(2,1)S(1)}) conditional(s32[]{:T(128)} %convert_element_type.119, (f32[8192,128]{1,0:T(8,128)}, f32[128,8192]{1,0:T(8,128)}) %tuple.66, (s32[2,12]{1,0:T(2,128)S(1)}, s32[]{:T(128)}, bf16[1,12,8,8192]{3,2,1,0:T(8,128)(2,1)}, pred[]{:T(512)}, ...), branch_computations={%region_1.1_spmd, %region_2.5_spmd} | conditional | flops 86523016 | bytes 102945120 | solution.py:102
  517.5 16.1 %conditional.7 = (f32[8192,128]{1,0:T(8,128)}, f32[128,8192]{1,0:T(8,128)}, bf16[8,8192]{1,0:T(8,128)(2,1)S(1)}) conditional(s32[]{:T(128)} %convert_element_type.120, (f32[8192,128]{1,0:T(8,128)}, f32[128,8192]{1,0:T(8,128)}) %tuple.68, (s32[2,12]{1,0:T(2,128)S(1)}, s32[]{:T(128)}, bf16[1,12,8,8192]{3,2,1,0:T(8,128)(2,1)}, pred[]{:T(512)}, ...), branch_computations={%region_6.6_spmd, %region_7.10_spmd} | conditional | flops 86523016 | bytes 102945120 | solution.py:102
  537.5 6.5 collective-permute-done.1
  544.0 17.3 %conditional.6 = (f32[8192,128]{1,0:T(8,128)}, f32[128,8192]{1,0:T(8,128)}, bf16[8,8192]{1,0:T(8,128)(2,1)S(1)}) conditional(s32[]{:T(128)} %convert_element_type.119, (f32[8192,128]{1,0:T(8,128)}, f32[128,8192]{1,0:T(8,128)}) %tuple.66, (s32[2,12]{1,0:T(2,128)S(1)}, s32[]{:T(128)}, bf16[1,12,8,8192]{3,2,1,0:T(8,128)(2,1)}, pred[]{:T(512)}, ...), branch_computations={%region_1.1_spmd, %region_2.5_spmd} | conditional | flops 86523016 | bytes 102945120 | solution.py:102
  563.3 16.1 %conditional.7 = (f32[8192,128]{1,0:T(8,128)}, f32[128,8192]{1,0:T(8,128)}, bf16[8,8192]{1,0:T(8,128)(2,1)S(1)}) conditional(s32[]{:T(128)} %convert_element_type.120, (f32[8192,128]{1,0:T(8,128)}, f32[128,8192]{1,0:T(8,128)}) %tuple.68, (s32[2,12]{1,0:T(2,128)S(1)}, s32[]{:T(128)}, bf16[1,12,8,8192]{3,2,1,0:T(8,128)(2,1)}, pred[]{:T(512)}, ...), branch_computations={%region_6.6_spmd, %region_7.10_spmd} | conditional | flops 86523016 | bytes 102945120 | solution.py:102
  583.2 6.5 collective-permute-done.1
  589.8 17.3 %conditional.6 = (f32[8192,128]{1,0:T(8,128)}, f32[128,8192]{1,0:T(8,128)}, bf16[8,8192]{1,0:T(8,128)(2,1)S(1)}) conditional(s32[]{:T(128)} %convert_element_type.119, (f32[8192,128]{1,0:T(8,128)}, f32[128,8192]{1,0:T(8,128)}) %tuple.66, (s32[2,12]{1,0:T(2,128)S(1)}, s32[]{:T(128)}, bf16[1,12,8,8192]{3,2,1,0:T(8,128)(2,1)}, pred[]{:T(512)}, ...), branch_computations={%region_1.1_spmd, %region_2.5_spmd} | conditional | flops 86523016 | bytes 102945120 | solution.py:102
  609.0 16.1 %conditional.7 = (f32[8192,128]{1,0:T(8,128)}, f32[128,8192]{1,0:T(8,128)}, bf16[8,8192]{1,0:T(8,128)(2,1)S(1)}) conditional(s32[]{:T(128)} %convert_element_type.120, (f32[8192,128]{1,0:T(8,128)}, f32[128,8192]{1,0:T(8,128)}) %tuple.68, (s32[2,12]{1,0:T(2,128)S(1)}, s32[]{:T(128)}, bf16[1,12,8,8192]{3,2,1,0:T(8,128)(2,1)}, pred[]{:T(512)}, ...), branch_computations={%region_6.6_spmd, %region_7.10_spmd} | conditional | flops 86523016 | bytes 102945120 | solution.py:102
  629.0 6.5 collective-permute-done.1
  635.6 17.3 %conditional.6 = (f32[8192,128]{1,0:T(8,128)}, f32[128,8192]{1,0:T(8,128)}, bf16[8,8192]{1,0:T(8,128)(2,1)S(1)}) conditional(s32[]{:T(128)} %convert_element_type.119, (f32[8192,128]{1,0:T(8,128)}, f32[128,8192]{1,0:T(8,128)}) %tuple.66, (s32[2,12]{1,0:T(2,128)S(1)}, s32[]{:T(128)}, bf16[1,12,8,8192]{3,2,1,0:T(8,128)(2,1)}, pred[]{:T(512)}, ...), branch_computations={%region_1.1_spmd, %region_2.5_spmd} | conditional | flops 86523016 | bytes 102945120 | solution.py:102
  654.8 16.1 %conditional.7 = (f32[8192,128]{1,0:T(8,128)}, f32[128,8192]{1,0:T(8,128)}, bf16[8,8192]{1,0:T(8,128)(2,1)S(1)}) conditional(s32[]{:T(128)} %convert_element_type.120, (f32[8192,128]{1,0:T(8,128)}, f32[128,8192]{1,0:T(8,128)}) %tuple.68, (s32[2,12]{1,0:T(2,128)S(1)}, s32[]{:T(128)}, bf16[1,12,8,8192]{3,2,1,0:T(8,128)(2,1)}, pred[]{:T(512)}, ...), branch_computations={%region_6.6_spmd, %region_7.10_spmd} | conditional | flops 86523016 | bytes 102945120 | solution.py:102
  674.8 6.5 collective-permute-done.1
  681.4 17.3 %conditional.6 = (f32[8192,128]{1,0:T(8,128)}, f32[128,8192]{1,0:T(8,128)}, bf16[8,8192]{1,0:T(8,128)(2,1)S(1)}) conditional(s32[]{:T(128)} %convert_element_type.119, (f32[8192,128]{1,0:T(8,128)}, f32[128,8192]{1,0:T(8,128)}) %tuple.66, (s32[2,12]{1,0:T(2,128)S(1)}, s32[]{:T(128)}, bf16[1,12,8,8192]{3,2,1,0:T(8,128)(2,1)}, pred[]{:T(512)}, ...), branch_computations={%region_1.1_spmd, %region_2.5_spmd} | conditional | flops 86523016 | bytes 102945120 | solution.py:102
  700.6 16.1 %conditional.7 = (f32[8192,128]{1,0:T(8,128)}, f32[128,8192]{1,0:T(8,128)}, bf16[8,8192]{1,0:T(8,128)(2,1)S(1)}) conditional(s32[]{:T(128)} %convert_element_type.120, (f32[8192,128]{1,0:T(8,128)}, f32[128,8192]{1,0:T(8,128)}) %tuple.68, (s32[2,12]{1,0:T(2,128)S(1)}, s32[]{:T(128)}, bf16[1,12,8,8192]{3,2,1,0:T(8,128)(2,1)}, pred[]{:T(512)}, ...), branch_computations={%region_6.6_spmd, %region_7.10_spmd} | conditional | flops 86523016 | bytes 102945120 | solution.py:102
  720.6 6.5 collective-permute-done.1
  727.2 17.3 %conditional.6 = (f32[8192,128]{1,0:T(8,128)}, f32[128,8192]{1,0:T(8,128)}, bf16[8,8192]{1,0:T(8,128)(2,1)S(1)}) conditional(s32[]{:T(128)} %convert_element_type.119, (f32[8192,128]{1,0:T(8,128)}, f32[128,8192]{1,0:T(8,128)}) %tuple.66, (s32[2,12]{1,0:T(2,128)S(1)}, s32[]{:T(128)}, bf16[1,12,8,8192]{3,2,1,0:T(8,128)(2,1)}, pred[]{:T(512)}, ...), branch_computations={%region_1.1_spmd, %region_2.5_spmd} | conditional | flops 86523016 | bytes 102945120 | solution.py:102
  746.4 16.1 %conditional.7 = (f32[8192,128]{1,0:T(8,128)}, f32[128,8192]{1,0:T(8,128)}, bf16[8,8192]{1,0:T(8,128)(2,1)S(1)}) conditional(s32[]{:T(128)} %convert_element_type.120, (f32[8192,128]{1,0:T(8,128)}, f32[128,8192]{1,0:T(8,128)}) %tuple.68, (s32[2,12]{1,0:T(2,128)S(1)}, s32[]{:T(128)}, bf16[1,12,8,8192]{3,2,1,0:T(8,128)(2,1)}, pred[]{:T(512)}, ...), branch_computations={%region_6.6_spmd, %region_7.10_spmd} | conditional | flops 86523016 | bytes 102945120 | solution.py:102
  766.4 6.5 collective-permute-done.1
  772.9 17.3 %conditional.6 = (f32[8192,128]{1,0:T(8,128)}, f32[128,8192]{1,0:T(8,128)}, bf16[8,8192]{1,0:T(8,128)(2,1)S(1)}) conditional(s32[]{:T(128)} %convert_element_type.119, (f32[8192,128]{1,0:T(8,128)}, f32[128,8192]{1,0:T(8,128)}) %tuple.66, (s32[2,12]{1,0:T(2,128)S(1)}, s32[]{:T(128)}, bf16[1,12,8,8192]{3,2,1,0:T(8,128)(2,1)}, pred[]{:T(512)}, ...), branch_computations={%region_1.1_spmd, %region_2.5_spmd} | conditional | flops 86523016 | bytes 102945120 | solution.py:102
  792.2 16.1 %conditional.7 = (f32[8192,128]{1,0:T(8,128)}, f32[128,8192]{1,0:T(8,128)}, bf16[8,8192]{1,0:T(8,128)(2,1)S(1)}) conditional(s32[]{:T(128)} %convert_element_type.120, (f32[8192,128]{1,0:T(8,128)}, f32[128,8192]{1,0:T(8,128)}) %tuple.68, (s32[2,12]{1,0:T(2,128)S(1)}, s32[]{:T(128)}, bf16[1,12,8,8192]{3,2,1,0:T(8,128)(2,1)}, pred[]{:T(512)}, ...), branch_computations={%region_6.6_spmd, %region_7.10_spmd} | conditional | flops 86523016 | bytes 102945120 | solution.py:102
  812.2 6.5 collective-permute-done.1
  818.7 17.3 %conditional.6 = (f32[8192,128]{1,0:T(8,128)}, f32[128,8192]{1,0:T(8,128)}, bf16[8,8192]{1,0:T(8,128)(2,1)S(1)}) conditional(s32[]{:T(128)} %convert_element_type.119, (f32[8192,128]{1,0:T(8,128)}, f32[128,8192]{1,0:T(8,128)}) %tuple.66, (s32[2,12]{1,0:T(2,128)S(1)}, s32[]{:T(128)}, bf16[1,12,8,8192]{3,2,1,0:T(8,128)(2,1)}, pred[]{:T(512)}, ...), branch_computations={%region_1.1_spmd, %region_2.5_spmd} | conditional | flops 86523016 | bytes 102945120 | solution.py:102
  838.0 16.1 %conditional.7 = (f32[8192,128]{1,0:T(8,128)}, f32[128,8192]{1,0:T(8,128)}, bf16[8,8192]{1,0:T(8,128)(2,1)S(1)}) conditional(s32[]{:T(128)} %convert_element_type.120, (f32[8192,128]{1,0:T(8,128)}, f32[128,8192]{1,0:T(8,128)}) %tuple.68, (s32[2,12]{1,0:T(2,128)S(1)}, s32[]{:T(128)}, bf16[1,12,8,8192]{3,2,1,0:T(8,128)(2,1)}, pred[]{:T(512)}, ...), branch_computations={%region_6.6_spmd, %region_7.10_spmd} | conditional | flops 86523016 | bytes 102945120 | solution.py:102
  858.0 6.5 collective-permute-done.1
  864.6 18.8 %collective-permute-start = (bf16[8,8192]{1,0:T(8,128)(2,1)S(1)}, bf16[8,8192]{1,0:T(8,128)(2,1)S(1)}, u32[]{:S(2)}, u32[]{:S(2)}) collective-permute-start(bf16[8,8192]{1,0:T(8,128)(2,1)S(1)} %get-tuple-element.853), channel_id=1, source_target_pairs={{16,0},{32,16},{48,32},{64,48},{80,64},{96,80},{112,96},{128,112},... | collective-permute-start | bytes 393224 | tf_op jit(solution)/shard_map/while/body/eval_jaxpr/ppermute | solution.py:16
  883.4 16.1 %conditional.7 = (f32[8192,128]{1,0:T(8,128)}, f32[128,8192]{1,0:T(8,128)}, bf16[8,8192]{1,0:T(8,128)(2,1)S(1)}) conditional(s32[]{:T(128)} %convert_element_type.120, (f32[8192,128]{1,0:T(8,128)}, f32[128,8192]{1,0:T(8,128)}) %tuple.68, (s32[2,12]{1,0:T(2,128)S(1)}, s32[]{:T(128)}, bf16[1,12,8,8192]{3,2,1,0:T(8,128)(2,1)}, pred[]{:T(512)}, ...), branch_computations={%region_6.6_spmd, %region_7.10_spmd} | conditional | flops 86523016 | bytes 102945120 | solution.py:102
  901.3 8.5 collective-permute-done.1
  911.9 19.9 %collective-permute-start.1 = (bf16[8,8192]{1,0:T(8,128)(2,1)S(1)}, bf16[8,8192]{1,0:T(8,128)(2,1)S(1)}, u32[]{:S(2)}, u32[]{:S(2)}) collective-permute-start(bf16[8,8192]{1,0:T(8,128)(2,1)S(1)} %get-tuple-element.854), channel_id=1, source_target_pairs={{0,16},{16,32},{32,48},{48,64},{64,80},{80,96},{96,112},{112,128},... | collective-permute-start | bytes 393224 | tf_op jit(solution)/shard_map/while/body/eval_jaxpr/ppermute | solution.py:16
  948.9 16.3 %collective-permute-start.1 = (bf16[8,8192]{1,0:T(8,128)(2,1)S(1)}, bf16[8,8192]{1,0:T(8,128)(2,1)S(1)}, u32[]{:S(2)}, u32[]{:S(2)}) collective-permute-start(bf16[8,8192]{1,0:T(8,128)(2,1)S(1)} %get-tuple-element.854), channel_id=1, source_target_pairs={{0,16},{16,32},{32,48},{48,64},{64,80},{80,96},{96,112},{112,128},... | collective-permute-start | bytes 393224 | tf_op jit(solution)/shard_map/while/body/eval_jaxpr/ppermute | solution.py:16
  982.2 16.3 %collective-permute-start.1 = (bf16[8,8192]{1,0:T(8,128)(2,1)S(1)}, bf16[8,8192]{1,0:T(8,128)(2,1)S(1)}, u32[]{:S(2)}, u32[]{:S(2)}) collective-permute-start(bf16[8,8192]{1,0:T(8,128)(2,1)S(1)} %get-tuple-element.854), channel_id=1, source_target_pairs={{0,16},{16,32},{32,48},{48,64},{64,80},{80,96},{96,112},{112,128},... | collective-permute-start | bytes 393224 | tf_op jit(solution)/shard_map/while/body/eval_jaxpr/ppermute | solution.py:16
  1016.1 17.7 %collective-permute-start.1 = (bf16[8,8192]{1,0:T(8,128)(2,1)S(1)}, bf16[8,8192]{1,0:T(8,128)(2,1)S(1)}, u32[]{:S(2)}, u32[]{:S(2)}) collective-permute-start(bf16[8,8192]{1,0:T(8,128)(2,1)S(1)} %get-tuple-element.854), channel_id=1, source_target_pairs={{0,16},{16,32},{32,48},{48,64},{64,80},{80,96},{96,112},{112,128},... | collective-permute-start | bytes 393224 | tf_op jit(solution)/shard_map/while/body/eval_jaxpr/ppermute | solution.py:16
  1051.6 109.7 %reduce-scatter.7.cloned.1.call-done = bf16[512,128]{1,0:T(8,128)(2,1)} async-done(((bf16[8192,128]{1,0:T(8,128)(2,1)}), bf16[512,128]{1,0:T(8,128)(2,1)}) %reduce-scatter.7.cloned.1.call-update) | async-done | bytes 131088 | tf_op jit(solution)/shard_map/reduce_scatter | solution.py:205
  1162.3 66.8 %reduce-scatter.9.cloned.1.call-done = bf16[128,512]{1,0:T(8,128)(2,1)} async-done(((bf16[128,8192]{1,0:T(8,128)(2,1)}), bf16[128,512]{1,0:T(8,128)(2,1)}) %reduce-scatter.9.cloned.1.call-update) | async-done | bytes 131088 | tf_op jit(solution)/shard_map/reduce_scatter | solution.py:208
  1231.8 6.6 collective-permute-done.6
  1240.6 13.5 collective-permute-done.7
  1259.4 7.8 collective-permute-done.8
  1268.1 8.4 collective-permute-done.9
  1276.6 21.2 %reduce-scatter.11.cloned.1.call-done = bf16[128,512]{1,0:T(8,128)(2,1)} async-done(((bf16[128,8192]{1,0:T(8,128)(2,1)}), bf16[128,512]{1,0:T(8,128)(2,1)}) %reduce-scatter.11.cloned.1.call-update) | async-done | bytes 131088 | tf_op jit(solution)/shard_map/reduce_scatter | solution.py:202
  1299.4 66.8 %reduce-scatter.5.cloned.1.call-done = bf16[512,128]{1,0:T(8,128)(2,1)} async-done(((bf16[8192,128]{1,0:T(8,128)(2,1)}), bf16[512,128]{1,0:T(8,128)(2,1)}) %reduce-scatter.5.cloned.1.call-update) | async-done | bytes 131088 | tf_op jit(solution)/shard_map/reduce_scatter | solution.py:199
  (803 shorter events, 605.1 us)
Async XLA Ops:
  7.2 91.9 %all-gather.9.cloned.1.call-start = ((), (), s32[]{:S(2)}) async-start(), calls=%async_computation.10 | async-start | bytes 2228224 | tf_op jit(solution)/shard_map/all_gather | solution.py:132
  7.9 93.9 %all-gather.7.cloned.1.call-start = ((), (), s32[]{:S(2)}) async-start(), calls=%async_computation.9 | async-start | bytes 2228224 | tf_op jit(solution)/shard_map/all_gather | solution.py:133
  8.6 135.4 %all-gather.11.cloned.1.call-start = ((), (), s32[]{:S(2)}) async-start(), calls=%async_computation.11 | async-start | bytes 2228224 | tf_op jit(solution)/shard_map/all_gather | solution.py:145
  10.6 8.3 collective-permute-start.2
  18.9 14.5 %collective-permute-start.3 = (bf16[2,128,512]{2,1,0:T(8,128)(2,1)S(1)}, bf16[2,128,512]{2,1,0:T(8,128)(2,1)S(1)}, u32[]{:S(2)}, u32[]{:S(2)}) collective-permute-start(bf16[2,128,512]{2,1,0:T(8,128)(2,1)S(1)} %collective-permute-done.2), channel_id=1, source_target_pairs={{0,32},{16,48},{32,0},{48,16},{64,96},{80,112},{96,64},{112,80},{1... | collective-permute-start | bytes 786440 | tf_op jit(solution)/shard_map/ppermute | solution.py:10
  33.4 17.9 %collective-permute-start.4 = (bf16[2,128,512]{2,1,0:T(8,128)(2,1)S(1)}, bf16[2,128,512]{2,1,0:T(8,128)(2,1)S(1)}, u32[]{:S(2)}, u32[]{:S(2)}) collective-permute-start(bf16[2,128,512]{2,1,0:T(8,128)(2,1)S(1)} %collective-permute-done.3), channel_id=1, source_target_pairs={{0,64},{16,80},{32,96},{48,112},{64,0},{80,16},{96,32},{112,48},{1... | collective-permute-start | bytes 786440 | tf_op jit(solution)/shard_map/ppermute | solution.py:10
  51.4 7.9 collective-permute-start.5
  61.8 37.2 %all-to-all-start = ((bf16[16,512,128]{2,1,0:T(8,128)(2,1)}), bf16[16,512,128]{2,1,0:T(8,128)(2,1)S(1)}, u32[]{:S(2)}, u32[]{:S(2)}) async-start(bf16[16,512,128]{2,1,0:T(8,128)(2,1)} %stack.15), calls=%async_computation | async-start | bytes 4194304 | tf_op jit(solution)/shard_map/all_to_all | solution.py:137
  67.1 1094.2 %reduce-scatter.7.cloned.1.call-start = ((), (), s32[]{:S(2)}) async-start(), calls=%async_computation.6 | async-start | bytes 2228224 | tf_op jit(solution)/shard_map/reduce_scatter | solution.py:205
  153.4 8.5 collective-permute-start
  158.9 10.9 collective-permute-start.1
  171.7 10.5 collective-permute-start.1
  184.2 10.5 collective-permute-start.1
  196.7 10.5 collective-permute-start.1
  209.2 20.0 %collective-permute-start.1 = (bf16[8,8192]{1,0:T(8,128)(2,1)S(1)}, bf16[8,8192]{1,0:T(8,128)(2,1)S(1)}, u32[]{:S(2)}, u32[]{:S(2)}) collective-permute-start(bf16[8,8192]{1,0:T(8,128)(2,1)S(1)} %get-tuple-element.854), channel_id=1, source_target_pairs={{0,16},{16,32},{32,48},{48,64},{64,80},{80,96},{96,112},{112,128},... | collective-permute-start | bytes 393224 | tf_op jit(solution)/shard_map/while/body/eval_jaxpr/ppermute | solution.py:16
  229.2 22.2 %collective-permute-start = (bf16[8,8192]{1,0:T(8,128)(2,1)S(1)}, bf16[8,8192]{1,0:T(8,128)(2,1)S(1)}, u32[]{:S(2)}, u32[]{:S(2)}) collective-permute-start(bf16[8,8192]{1,0:T(8,128)(2,1)S(1)} %get-tuple-element.853), channel_id=1, source_target_pairs={{16,0},{32,16},{48,32},{64,48},{80,64},{96,80},{112,96},{128,112},... | collective-permute-start | bytes 393224 | tf_op jit(solution)/shard_map/while/body/eval_jaxpr/ppermute | solution.py:16
  249.0 22.9 %collective-permute-start.1 = (bf16[8,8192]{1,0:T(8,128)(2,1)S(1)}, bf16[8,8192]{1,0:T(8,128)(2,1)S(1)}, u32[]{:S(2)}, u32[]{:S(2)}) collective-permute-start(bf16[8,8192]{1,0:T(8,128)(2,1)S(1)} %get-tuple-element.854), channel_id=1, source_target_pairs={{0,16},{16,32},{32,48},{48,64},{64,80},{80,96},{96,112},{112,128},... | collective-permute-start | bytes 393224 | tf_op jit(solution)/shard_map/while/body/eval_jaxpr/ppermute | solution.py:16
  271.9 55.4 %collective-permute-start = (bf16[8,8192]{1,0:T(8,128)(2,1)S(1)}, bf16[8,8192]{1,0:T(8,128)(2,1)S(1)}, u32[]{:S(2)}, u32[]{:S(2)}) collective-permute-start(bf16[8,8192]{1,0:T(8,128)(2,1)S(1)} %get-tuple-element.853), channel_id=1, source_target_pairs={{16,0},{32,16},{48,32},{64,48},{80,64},{96,80},{112,96},{128,112},... | collective-permute-start | bytes 393224 | tf_op jit(solution)/shard_map/while/body/eval_jaxpr/ppermute | solution.py:16
  291.9 37.0 %collective-permute-start.1 = (bf16[8,8192]{1,0:T(8,128)(2,1)S(1)}, bf16[8,8192]{1,0:T(8,128)(2,1)S(1)}, u32[]{:S(2)}, u32[]{:S(2)}) collective-permute-start(bf16[8,8192]{1,0:T(8,128)(2,1)S(1)} %get-tuple-element.854), channel_id=1, source_target_pairs={{0,16},{16,32},{32,48},{48,64},{64,80},{80,96},{96,112},{112,128},... | collective-permute-start | bytes 393224 | tf_op jit(solution)/shard_map/while/body/eval_jaxpr/ppermute | solution.py:16
  346.2 8.5 collective-permute-start
  348.2 10.7 collective-permute-start.1
  376.2 21.9 %collective-permute-start = (bf16[8,8192]{1,0:T(8,128)(2,1)S(1)}, bf16[8,8192]{1,0:T(8,128)(2,1)S(1)}, u32[]{:S(2)}, u32[]{:S(2)}) collective-permute-start(bf16[8,8192]{1,0:T(8,128)(2,1)S(1)} %get-tuple-element.853), channel_id=1, source_target_pairs={{16,0},{32,16},{48,32},{64,48},{80,64},{96,80},{112,96},{128,112},... | collective-permute-start | bytes 393224 | tf_op jit(solution)/shard_map/while/body/eval_jaxpr/ppermute | solution.py:16
  396.2 10.5 collective-permute-start.1
  424.0 21.9 %collective-permute-start = (bf16[8,8192]{1,0:T(8,128)(2,1)S(1)}, bf16[8,8192]{1,0:T(8,128)(2,1)S(1)}, u32[]{:S(2)}, u32[]{:S(2)}) collective-permute-start(bf16[8,8192]{1,0:T(8,128)(2,1)S(1)} %get-tuple-element.853), channel_id=1, source_target_pairs={{16,0},{32,16},{48,32},{64,48},{80,64},{96,80},{112,96},{128,112},... | collective-permute-start | bytes 393224 | tf_op jit(solution)/shard_map/while/body/eval_jaxpr/ppermute | solution.py:16
  441.9 10.5 collective-permute-start.1
  469.7 21.9 %collective-permute-start = (bf16[8,8192]{1,0:T(8,128)(2,1)S(1)}, bf16[8,8192]{1,0:T(8,128)(2,1)S(1)}, u32[]{:S(2)}, u32[]{:S(2)}) collective-permute-start(bf16[8,8192]{1,0:T(8,128)(2,1)S(1)} %get-tuple-element.853), channel_id=1, source_target_pairs={{16,0},{32,16},{48,32},{64,48},{80,64},{96,80},{112,96},{128,112},... | collective-permute-start | bytes 393224 | tf_op jit(solution)/shard_map/while/body/eval_jaxpr/ppermute | solution.py:16
  487.7 10.5 collective-permute-start.1
  515.5 21.9 %collective-permute-start = (bf16[8,8192]{1,0:T(8,128)(2,1)S(1)}, bf16[8,8192]{1,0:T(8,128)(2,1)S(1)}, u32[]{:S(2)}, u32[]{:S(2)}) collective-permute-start(bf16[8,8192]{1,0:T(8,128)(2,1)S(1)} %get-tuple-element.853), channel_id=1, source_target_pairs={{16,0},{32,16},{48,32},{64,48},{80,64},{96,80},{112,96},{128,112},... | collective-permute-start | bytes 393224 | tf_op jit(solution)/shard_map/while/body/eval_jaxpr/ppermute | solution.py:16
  533.5 10.5 collective-permute-start.1
  561.3 21.9 %collective-permute-start = (bf16[8,8192]{1,0:T(8,128)(2,1)S(1)}, bf16[8,8192]{1,0:T(8,128)(2,1)S(1)}, u32[]{:S(2)}, u32[]{:S(2)}) collective-permute-start(bf16[8,8192]{1,0:T(8,128)(2,1)S(1)} %get-tuple-element.853), channel_id=1, source_target_pairs={{16,0},{32,16},{48,32},{64,48},{80,64},{96,80},{112,96},{128,112},... | collective-permute-start | bytes 393224 | tf_op jit(solution)/shard_map/while/body/eval_jaxpr/ppermute | solution.py:16
  579.3 10.5 collective-permute-start.1
  607.1 21.9 %collective-permute-start = (bf16[8,8192]{1,0:T(8,128)(2,1)S(1)}, bf16[8,8192]{1,0:T(8,128)(2,1)S(1)}, u32[]{:S(2)}, u32[]{:S(2)}) collective-permute-start(bf16[8,8192]{1,0:T(8,128)(2,1)S(1)} %get-tuple-element.853), channel_id=1, source_target_pairs={{16,0},{32,16},{48,32},{64,48},{80,64},{96,80},{112,96},{128,112},... | collective-permute-start | bytes 393224 | tf_op jit(solution)/shard_map/while/body/eval_jaxpr/ppermute | solution.py:16
  625.1 10.5 collective-permute-start.1
  652.9 21.9 %collective-permute-start = (bf16[8,8192]{1,0:T(8,128)(2,1)S(1)}, bf16[8,8192]{1,0:T(8,128)(2,1)S(1)}, u32[]{:S(2)}, u32[]{:S(2)}) collective-permute-start(bf16[8,8192]{1,0:T(8,128)(2,1)S(1)} %get-tuple-element.853), channel_id=1, source_target_pairs={{16,0},{32,16},{48,32},{64,48},{80,64},{96,80},{112,96},{128,112},... | collective-permute-start | bytes 393224 | tf_op jit(solution)/shard_map/while/body/eval_jaxpr/ppermute | solution.py:16
  670.9 10.5 collective-permute-start.1
  698.7 21.9 %collective-permute-start = (bf16[8,8192]{1,0:T(8,128)(2,1)S(1)}, bf16[8,8192]{1,0:T(8,128)(2,1)S(1)}, u32[]{:S(2)}, u32[]{:S(2)}) collective-permute-start(bf16[8,8192]{1,0:T(8,128)(2,1)S(1)} %get-tuple-element.853), channel_id=1, source_target_pairs={{16,0},{32,16},{48,32},{64,48},{80,64},{96,80},{112,96},{128,112},... | collective-permute-start | bytes 393224 | tf_op jit(solution)/shard_map/while/body/eval_jaxpr/ppermute | solution.py:16
  716.7 10.5 collective-permute-start.1
  744.5 21.9 %collective-permute-start = (bf16[8,8192]{1,0:T(8,128)(2,1)S(1)}, bf16[8,8192]{1,0:T(8,128)(2,1)S(1)}, u32[]{:S(2)}, u32[]{:S(2)}) collective-permute-start(bf16[8,8192]{1,0:T(8,128)(2,1)S(1)} %get-tuple-element.853), channel_id=1, source_target_pairs={{16,0},{32,16},{48,32},{64,48},{80,64},{96,80},{112,96},{128,112},... | collective-permute-start | bytes 393224 | tf_op jit(solution)/shard_map/while/body/eval_jaxpr/ppermute | solution.py:16
  762.5 10.5 collective-permute-start.1
  790.3 21.9 %collective-permute-start = (bf16[8,8192]{1,0:T(8,128)(2,1)S(1)}, bf16[8,8192]{1,0:T(8,128)(2,1)S(1)}, u32[]{:S(2)}, u32[]{:S(2)}) collective-permute-start(bf16[8,8192]{1,0:T(8,128)(2,1)S(1)} %get-tuple-element.853), channel_id=1, source_target_pairs={{16,0},{32,16},{48,32},{64,48},{80,64},{96,80},{112,96},{128,112},... | collective-permute-start | bytes 393224 | tf_op jit(solution)/shard_map/while/body/eval_jaxpr/ppermute | solution.py:16
  808.3 10.5 collective-permute-start.1
  836.1 21.9 %collective-permute-start = (bf16[8,8192]{1,0:T(8,128)(2,1)S(1)}, bf16[8,8192]{1,0:T(8,128)(2,1)S(1)}, u32[]{:S(2)}, u32[]{:S(2)}) collective-permute-start(bf16[8,8192]{1,0:T(8,128)(2,1)S(1)} %get-tuple-element.853), channel_id=1, source_target_pairs={{16,0},{32,16},{48,32},{64,48},{80,64},{96,80},{112,96},{128,112},... | collective-permute-start | bytes 393224 | tf_op jit(solution)/shard_map/while/body/eval_jaxpr/ppermute | solution.py:16
  854.1 10.5 collective-permute-start.1
  864.6 36.8 %collective-permute-start = (bf16[8,8192]{1,0:T(8,128)(2,1)S(1)}, bf16[8,8192]{1,0:T(8,128)(2,1)S(1)}, u32[]{:S(2)}, u32[]{:S(2)}) collective-permute-start(bf16[8,8192]{1,0:T(8,128)(2,1)S(1)} %get-tuple-element.853), channel_id=1, source_target_pairs={{16,0},{32,16},{48,32},{64,48},{80,64},{96,80},{112,96},{128,112},... | collective-permute-start | bytes 393224 | tf_op jit(solution)/shard_map/while/body/eval_jaxpr/ppermute | solution.py:16
  899.4 10.5 collective-permute-start.1
  909.9 21.9 %collective-permute-start = (bf16[8,8192]{1,0:T(8,128)(2,1)S(1)}, bf16[8,8192]{1,0:T(8,128)(2,1)S(1)}, u32[]{:S(2)}, u32[]{:S(2)}) collective-permute-start(bf16[8,8192]{1,0:T(8,128)(2,1)S(1)} %get-tuple-element.853), channel_id=1, source_target_pairs={{16,0},{32,16},{48,32},{64,48},{80,64},{96,80},{112,96},{128,112},... | collective-permute-start | bytes 393224 | tf_op jit(solution)/shard_map/while/body/eval_jaxpr/ppermute | solution.py:16
  911.9 22.4 %collective-permute-start.1 = (bf16[8,8192]{1,0:T(8,128)(2,1)S(1)}, bf16[8,8192]{1,0:T(8,128)(2,1)S(1)}, u32[]{:S(2)}, u32[]{:S(2)}) collective-permute-start(bf16[8,8192]{1,0:T(8,128)(2,1)S(1)} %get-tuple-element.854), channel_id=1, source_target_pairs={{0,16},{16,32},{32,48},{48,64},{64,80},{80,96},{96,112},{112,128},... | collective-permute-start | bytes 393224 | tf_op jit(solution)/shard_map/while/body/eval_jaxpr/ppermute | solution.py:16
  936.4 10.5 collective-permute-start.1
  946.9 19.3 %collective-permute-start = (bf16[8,8192]{1,0:T(8,128)(2,1)S(1)}, bf16[8,8192]{1,0:T(8,128)(2,1)S(1)}, u32[]{:S(2)}, u32[]{:S(2)}) collective-permute-start(bf16[8,8192]{1,0:T(8,128)(2,1)S(1)} %get-tuple-element.853), channel_id=1, source_target_pairs={{16,0},{32,16},{48,32},{64,48},{80,64},{96,80},{112,96},{128,112},... | collective-permute-start | bytes 393224 | tf_op jit(solution)/shard_map/while/body/eval_jaxpr/ppermute | solution.py:16
  948.9 18.8 %collective-permute-start.1 = (bf16[8,8192]{1,0:T(8,128)(2,1)S(1)}, bf16[8,8192]{1,0:T(8,128)(2,1)S(1)}, u32[]{:S(2)}, u32[]{:S(2)}) collective-permute-start(bf16[8,8192]{1,0:T(8,128)(2,1)S(1)} %get-tuple-element.854), channel_id=1, source_target_pairs={{0,16},{16,32},{32,48},{48,64},{64,80},{80,96},{96,112},{112,128},... | collective-permute-start | bytes 393224 | tf_op jit(solution)/shard_map/while/body/eval_jaxpr/ppermute | solution.py:16
  969.7 10.5 collective-permute-start.1
  980.2 19.3 %collective-permute-start = (bf16[8,8192]{1,0:T(8,128)(2,1)S(1)}, bf16[8,8192]{1,0:T(8,128)(2,1)S(1)}, u32[]{:S(2)}, u32[]{:S(2)}) collective-permute-start(bf16[8,8192]{1,0:T(8,128)(2,1)S(1)} %get-tuple-element.853), channel_id=1, source_target_pairs={{16,0},{32,16},{48,32},{64,48},{80,64},{96,80},{112,96},{128,112},... | collective-permute-start | bytes 393224 | tf_op jit(solution)/shard_map/while/body/eval_jaxpr/ppermute | solution.py:16
  982.2 18.8 %collective-permute-start.1 = (bf16[8,8192]{1,0:T(8,128)(2,1)S(1)}, bf16[8,8192]{1,0:T(8,128)(2,1)S(1)}, u32[]{:S(2)}, u32[]{:S(2)}) collective-permute-start(bf16[8,8192]{1,0:T(8,128)(2,1)S(1)} %get-tuple-element.854), channel_id=1, source_target_pairs={{0,16},{16,32},{32,48},{48,64},{64,80},{80,96},{96,112},{112,128},... | collective-permute-start | bytes 393224 | tf_op jit(solution)/shard_map/while/body/eval_jaxpr/ppermute | solution.py:16
  1001.1 7.5 collective-permute-start
  1003.6 10.5 collective-permute-start.1
  1014.1 20.6 %collective-permute-start = (bf16[8,8192]{1,0:T(8,128)(2,1)S(1)}, bf16[8,8192]{1,0:T(8,128)(2,1)S(1)}, u32[]{:S(2)}, u32[]{:S(2)}) collective-permute-start(bf16[8,8192]{1,0:T(8,128)(2,1)S(1)} %get-tuple-element.853), channel_id=1, source_target_pairs={{16,0},{32,16},{48,32},{64,48},{80,64},{96,80},{112,96},{128,112},... | collective-permute-start | bytes 393224 | tf_op jit(solution)/shard_map/while/body/eval_jaxpr/ppermute | solution.py:16
  1016.1 20.2 %collective-permute-start.1 = (bf16[8,8192]{1,0:T(8,128)(2,1)S(1)}, bf16[8,8192]{1,0:T(8,128)(2,1)S(1)}, u32[]{:S(2)}, u32[]{:S(2)}) collective-permute-start(bf16[8,8192]{1,0:T(8,128)(2,1)S(1)} %get-tuple-element.854), channel_id=1, source_target_pairs={{0,16},{16,32},{32,48},{48,64},{64,80},{80,96},{96,112},{112,128},... | collective-permute-start | bytes 393224 | tf_op jit(solution)/shard_map/while/body/eval_jaxpr/ppermute | solution.py:16
  1040.0 189.1 %reduce-scatter.9.cloned.1.call-start = ((), (), s32[]{:S(2)}) async-start(), calls=%async_computation.7 | async-start | bytes 2228224 | tf_op jit(solution)/shard_map/reduce_scatter | solution.py:208
  1043.9 253.9 %reduce-scatter.11.cloned.1.call-start = ((), (), s32[]{:S(2)}) async-start(), calls=%async_computation.8 | async-start | bytes 2228224 | tf_op jit(solution)/shard_map/reduce_scatter | solution.py:202
  1047.8 318.4 %reduce-scatter.5.cloned.1.call-start = ((), (), s32[]{:S(2)}) async-start(), calls=%async_computation.5 | async-start | bytes 2228224 | tf_op jit(solution)/shard_map/reduce_scatter | solution.py:199
  1230.1 8.4 collective-permute-start.6
  1238.4 15.7 %collective-permute-start.7 = (bf16[2,128,512]{2,1,0:T(8,128)(2,1)S(1)}, bf16[2,128,512]{2,1,0:T(8,128)(2,1)S(1)}, u32[]{:S(2)}, u32[]{:S(2)}) collective-permute-start(bf16[2,128,512]{2,1,0:T(8,128)(2,1)S(1)} %collective-permute-done.6), channel_id=1, source_target_pairs={{0,32},{16,48},{32,0},{48,16},{64,96},{80,112},{96,64},{112,80},{1... | collective-permute-start | bytes 786440 | tf_op jit(solution)/shard_map/ppermute | solution.py:10
  1254.1 13.1 collective-permute-start.8
  1267.2 9.3 collective-permute-start.9
  (130 other events, 394.7 us)
Sparse Core Ops, SparseCore 0:
  9.8 38.6 all-gather.8
  50.3 51.4 all-gather.6
  104.2 39.7 all-gather.10
  1040.1 121.1 reduce-scatter.6
  1163.7 65.3 reduce-scatter.8
  1231.5 66.2 reduce-scatter.10
  1300.3 65.8 reduce-scatter.4
